TPU v7x, 512 devices: a whole 4x4x16 slice. The times are simulated.
512 devices in a mesh: tile: 128 (over x, z, y_lo), layer: 4 (over y_hi, core).
Axes of the slice: x: 4, y: 4 (y_hi: 2, y_lo: 2; y = y_hi * 2 + y_lo), z: 16, core: 2. Of those that a mesh axis runs over, the one named last changes fastest.
Arguments:
- probes: float32 [8, 3, 8, 1024, 128], P(None, None, 'layer', 'tile'), may hold values from -46 to 46
- material: int32 [8, 1024, 128], P('layer', 'tile'), may hold values from 0 to 2
- lame_pairs: float32 [3, 2], replicated, may hold values from 0.5 to 5
Outputs:
- solution: float32 [8, 3, 8, 1024, 128], P(None, None, 'layer', 'tile')
- residual: float32 [8, 3, 8, 1024, 128], P(None, None, 'layer', 'tile')
Inputs may be any that keep to these rules, and one draw needn't show every extreme that they name: `material`: 0 die silicon, 1 copper, 2 underfill.
All inputs are finite; a program needn't handle non-finite values.
Results may differ from a plain program's by a relative error of at most 0.0003.
Values sent between devices are 32-bit elements; how exact they have to be, the bound alone decides.
No kernel may reach another device: no remote copies, remote signals or barrier semaphores. Data moves between devices by JAX's collectives and lax.ppermute only.
A program may use at most 64 MiB of HBM per device.

v0:
```python
import math

import jax
import jax.numpy as jnp
import numpy as np
from jax import lax
from jax.sharding import Mesh
from jax.sharding import PartitionSpec as P

ITERS = 2
TILE = ("tile_0", "tile_1", "tile_2")
LAYER = ("layer_0", "layer_1")
TILE_LAYER = ("tile_0", "tile_1", "tile_2", "layer_0", "layer_1")


def from_behind(array, axis, by):
    peers = lax.axis_size(axis)
    pairs = [(i, i + by) for i in range(peers) if 0 <= i + by < peers]
    return lax.ppermute(array, axis, pairs)


def one_axis_at_a_time(array, axes):
    for axis in axes:
        array = lax.psum(array, axis)
    return array


def element_tables():
    points = [0.5 - 0.5 / math.sqrt(3.0), 0.5 + 0.5 / math.sqrt(3.0)]
    offsets = (
        np.array([[corner >> 2 & 1, corner >> 1 & 1, corner & 1] for corner in range(8)]) * 1.0
    )
    identity = np.eye(3)
    lam_table = np.zeros((24, 24))
    mu_table = np.zeros((24, 24))
    for point_one in points:
        for point_two in points:
            for point_three in points:
                location = np.array([point_one, point_two, point_three])
                factors = np.where(offsets > 0.5, location, 1.0 - location)
                slopes = np.where(offsets > 0.5, 1.0, -1.0)
                gradients = np.zeros((8, 3))
                for coordinate in range(3):
                    others = factors.copy()
                    others[:, coordinate] = slopes[:, coordinate]
                    gradients[:, coordinate] = np.prod(others, axis=1)
                outer = gradients[:, :, None, None] * gradients[None, None, :, :]
                lam_table += 0.125 * outer.reshape(24, 24)
                gradient_dots = gradients @ gradients.T
                first_term = gradient_dots[:, None, :, None] * identity[None, :, None, :]
                second_term = gradients[:, None, None, :] * gradients.T[None, :, :, None]
                mu_table += 0.125 * (first_term + second_term).reshape(24, 24)
    return np.concatenate([lam_table, mu_table], 1).astype(np.float32)


def material_fields(material, lame_pairs):
    lam_cells = jnp.zeros(material.shape, jnp.float32)
    mu_cells = jnp.zeros(material.shape, jnp.float32)
    for kind_index in range(lame_pairs.shape[0]):
        chosen = material == kind_index
        lam_cells = lam_cells + jnp.where(chosen, lame_pairs[kind_index, 0], 0.0)
        mu_cells = mu_cells + jnp.where(chosen, lame_pairs[kind_index, 1], 0.0)
    return (lam_cells, mu_cells)


def element_forces(single, lam_cells, mu_cells, tables):
    depth_cells, width_cells, span_cells = lam_cells.shape
    cell_count = depth_cells * width_cells * span_cells
    pieces = []
    for corner in range(8):
        up_depth = corner >> 2 & 1
        up_width = corner >> 1 & 1
        up_span = corner & 1
        sliced = single[:, up_depth : up_depth + depth_cells, up_width : up_width + width_cells, :]
        if up_span:
            sliced = jnp.concatenate([sliced[..., 1:], jnp.zeros_like(sliced[..., :1])], -1)
        pieces.append(sliced.reshape(3, cell_count))
    stacked = jnp.concatenate(pieces, 0)
    scaled = jnp.concatenate(
        [stacked * lam_cells.reshape(1, cell_count), stacked * mu_cells.reshape(1, cell_count)], 0
    )
    forces = jnp.dot(
        tables, scaled, precision=lax.Precision.HIGHEST, preferred_element_type=jnp.float32
    )
    forces = forces.reshape(8, 3, depth_cells, width_cells, span_cells)
    summed = jnp.zeros((3, depth_cells + 1, width_cells + 1, span_cells), jnp.float32)
    for corner in range(8):
        up_depth = corner >> 2 & 1
        up_width = corner >> 1 & 1
        up_span = corner & 1
        contrib = forces[corner]
        if up_span:
            contrib = jnp.concatenate([jnp.zeros_like(contrib[..., :1]), contrib[..., :-1]], -1)
        summed = summed + jnp.pad(
            contrib, ((0, 0), (up_depth, 1 - up_depth), (up_width, 1 - up_width), (0, 0))
        )
    return summed


def pull_tile(values):
    arrived = from_behind(values[:, :, :, 0:1, :], TILE, -1)
    return jnp.concatenate([values, arrived], 3)


def pull_layer(values):
    arrived = from_behind(values[:, :, 0:1], LAYER, -1)
    return jnp.concatenate([values, arrived], 2)


def push_layer(values):
    arrived = from_behind(values[:, :, -1:], LAYER, 1)
    return jnp.concatenate([values[:, :, 0:1] + arrived, values[:, :, 1:-1]], 2)


def push_tile(values):
    arrived = from_behind(values[:, :, :, -1:], TILE, 1)
    return jnp.concatenate([values[:, :, :, 0:1] + arrived, values[:, :, :, 1:-1]], 3)


def stiffness_apply(nodal_values, lam_cells, mu_cells, tables):
    extended = pull_layer(pull_tile(nodal_values))
    forces = lax.map(lambda single: element_forces(single, lam_cells, mu_cells, tables), extended)
    return push_tile(push_layer(forces))


def local_gram(left_block, right_block):
    count_rows = left_block.shape[0]
    return jnp.dot(
        left_block.reshape(count_rows, -1),
        right_block.reshape(count_rows, -1).T,
        precision=lax.Precision.HIGHEST,
        preferred_element_type=jnp.float32,
    )


def small_product(left_matrix, right_matrix):
    return jnp.dot(
        left_matrix,
        right_matrix,
        precision=lax.Precision.HIGHEST,
        preferred_element_type=jnp.float32,
    )


def combine(coefficients, block_rows):
    count_rows = block_rows.shape[0]
    mixed = jnp.dot(
        coefficients.T,
        block_rows.reshape(count_rows, -1),
        precision=lax.Precision.HIGHEST,
        preferred_element_type=jnp.float32,
    )
    return mixed.reshape(block_rows.shape)


def spd_solve(matrix, right_side):
    lower_factor = jnp.linalg.cholesky(matrix)
    middle = lax.linalg.triangular_solve(lower_factor, right_side, left_side=True, lower=True)
    return lax.linalg.triangular_solve(
        lower_factor, middle, left_side=True, lower=True, transpose_a=True
    )


def symmetric(matrix):
    return 0.5 * (matrix + matrix.T)


def body(probes, material, lame_pairs):
    lam_cells, mu_cells = material_fields(material, lame_pairs)
    tables = jnp.asarray(element_tables(), jnp.float32)
    solution = jnp.zeros_like(probes)
    residual = probes
    direction = probes
    norms_now = symmetric(one_axis_at_a_time(local_gram(residual, residual), TILE_LAYER))
    for turn_index in range(ITERS):
        image_block = stiffness_apply(direction, lam_cells, mu_cells, tables)
        curvature, cross_gram, image_gram = (
            one_axis_at_a_time(local_gram(direction, image_block), TILE_LAYER),
            one_axis_at_a_time(local_gram(residual, image_block), TILE_LAYER),
            one_axis_at_a_time(local_gram(image_block, image_block), TILE_LAYER),
        )
        curvature = symmetric(curvature)
        step_alpha = spd_solve(curvature, norms_now)
        solution = solution + combine(step_alpha, direction)
        residual = residual - combine(step_alpha, image_block)
        if turn_index + 1 < ITERS:
            leaving = small_product(cross_gram, step_alpha)
            norms_next = (
                norms_now
                - leaving
                - leaving.T
                + small_product(step_alpha.T, small_product(image_gram, step_alpha))
            )
            norms_next = symmetric(norms_next)
        if turn_index + 1 < ITERS:
            step_beta = spd_solve(norms_now, norms_next)
            direction = residual + combine(step_beta, direction)
            norms_now = norms_next
    return (solution, residual)


def solution(mesh):
    split = Mesh(
        mesh.devices.reshape(4, 16, 2, 2, 2), ("tile_0", "tile_1", "tile_2", "layer_0", "layer_1")
    )
    placed = (P(None, None, LAYER, TILE, None), P(LAYER, TILE, None), P())
    return jax.shard_map(
        body,
        mesh=split,
        in_specs=placed,
        out_specs=(P(None, None, LAYER, TILE, None), P(None, None, LAYER, TILE, None)),
        check_vma=False,
    )
```

profile of v0, /device:TPU:1, one launch (start us, length us, event | category | flops | bytes accessed | tf_op | source)
XLA Modules:
  0.0 252.7 jit_solution(9410640632337662533)
XLA Ops:
  0.6 0.9 slice.346
  1.6 1.3 collective-permute-start
  2.9 0.7 fusion.65
  3.6 1.9 select_add_fusion
  5.5 0.9 constant_dynamic-update-slice_fusion
  7.0 9.2 %collective-permute-start.1 = (f32[8,3,1,9,128]{4,3,2,1,0:T(8,128)S(1)}, f32[8,3,1,9,128]{4,3,2,1,0:T(8,128)S(1)}, u32[]{:S(2)}, u32[]{:S(2)}) collective-permute-start(f32[8,3,1,9,128]{4,3,2,1,0:T(8,128)S(1)} %slice.492), channel_id=1, source_target_pairs={{1,0},{2,1},{3,2},{5,4},{6,5},{7,6},{9,8},{10,9},{11,10},{13,12},{... | collective-permute-start | bytes 331784 | tf_op jit(solution)/shard_map/ppermute | solution.py:19
  16.2 1.9 select_add_fusion.1
  18.2 0.7 copy-done.1
  18.9 15.1 %while.26 = (s32[]{:T(128)}, f32[8,3,3,9,128]{4,0,3,2,1:T(8,128)S(1)}, f32[8,3,3,9,128]{4,3,2,1,0:T(8,128)S(1)}, f32[2,8,128]{2,1,0:T(8,128)S(1)}, f32[2,8,128]{...) while((s32[]{:T(128)}, ...), condition=%wide.region_1.2_spmd.clone, body=%wide.region_0.1_spmd.sunk.clone.sunk | while | flops 28531584 | bytes 3650669 | solution.py:122
  34.0 1.9 collective-permute-start.2
  35.9 1.7 collective-permute-done.2
  37.7 3.6 %collective-permute-start.3 = (f32[8,3,2,1,128]{4,0,3,2,1:T(8,128)S(1)}, f32[8,3,2,1,128]{4,0,3,2,1:T(8,128)S(1)}, u32[]{:S(2)}, u32[]{:S(2)}) collective-permute-start(f32[8,3,2,1,128]{4,0,3,2,1:T(8,128)S(1)} %pad_maximum_fusion.4), channel_id=1, source_target_pairs={{0,4},{4,8},{8,12},{12,16},{16,20},{20,24},{24,28},{28,32},{32,36}... | collective-permute-start | bytes 73736 | tf_op jit(solution)/shard_map/ppermute | solution.py:19
  42.2 0.5 convolution_bitcast_fusion.5
  42.8 0.5 convolution_bitcast_fusion.3
  43.3 25.8 %all-reduce.33 = (f32[8,8]{0,1:T(8,128)S(1)}, f32[8,8]{1,0:T(8,128)S(1)}, f32[8,8]{1,0:T(8,128)S(1)}) all-reduce(f32[8,8]{0,1:T(8,128)S(1)} %convolution_bitcast_fusion.4, f32[8,8]{1,0:T(8,128)S(1)} %convolution_bitcast_fusion.5, ...), channel_id=1, replica_groups=mesh['tile_0'=4,'tile_1'=16,'tile_2'=2,'layer_0'=2,'layer_1'=2] {'tile_0'}, use_global_device_ids=true, to_apply=%region_9.11 | all-reduce | flops 192 | bytes 1536 | tf_op jit(solution)/shard_map/psum | solution.py:24
  69.1 39.1 %all-reduce.32 = (f32[8,8]{0,1:T(8,128)S(1)}, f32[8,8]{1,0:T(8,128)S(1)}, f32[8,8]{1,0:T(8,128)S(1)}) all-reduce(f32[8,8]{0,1:T(8,128)S(1)} %get-tuple-element.227, f32[8,8]{1,0:T(8,128)S(1)} %get-tuple-element.228, ...), channel_id=1, replica_groups=mesh['tile_0'=4,'tile_1'=16,'tile_2'=2,'layer_0'=2,'layer_1'=2] {'tile_1'}, use_global_device_ids=true, to_apply=%region_10.12 | all-reduce | flops 192 | bytes 1536 | tf_op jit(solution)/shard_map/psum | solution.py:24
  108.2 5.0 %all-reduce.36 = (f32[8,8]{0,1:T(8,128)S(1)}, f32[8,8]{1,0:T(8,128)S(1)}, f32[8,8]{1,0:T(8,128)S(1)}) all-reduce(f32[8,8]{0,1:T(8,128)S(1)} %get-tuple-element.224, f32[8,8]{1,0:T(8,128)S(1)} %get-tuple-element.225, ...), channel_id=1, replica_groups=mesh['tile_0'=4,'tile_1'=16,'tile_2'=2,'layer_0'=2,'layer_1'=2] {'tile_2'}, use_global_device_ids=true, to_apply=%region_11.13 | all-reduce | flops 192 | bytes 1536 | tf_op jit(solution)/shard_map/psum | solution.py:24
  113.2 6.5 %all-reduce.35 = (f32[8,8]{0,1:T(8,128)S(1)}, f32[8,8]{1,0:T(8,128)S(1)}, f32[8,8]{1,0:T(8,128)S(1)}) all-reduce(f32[8,8]{0,1:T(8,128)S(1)} %get-tuple-element.236, f32[8,8]{1,0:T(8,128)S(1)} %get-tuple-element.237, ...), channel_id=1, replica_groups=mesh['tile_0'=4,'tile_1'=16,'tile_2'=2,'layer_0'=2,'layer_1'=2] {'layer_0'}, use_global_device_ids=true, to_apply=%region_12.14 | all-reduce | flops 192 | bytes 1536 | tf_op jit(solution)/shard_map/psum | solution.py:24
  119.7 28.8 %all-reduce.34 = (f32[8,8]{0,1:T(8,128)S(1)}, f32[8,8]{1,0:T(8,128)S(1)}, f32[8,8]{1,0:T(8,128)S(1)}) all-reduce(f32[8,8]{0,1:T(8,128)S(1)} %get-tuple-element.233, f32[8,8]{1,0:T(8,128)S(1)} %get-tuple-element.234, ...), channel_id=1, replica_groups=mesh['tile_0'=4,'tile_1'=16,'tile_2'=2,'layer_0'=2,'layer_1'=2] {'layer_1'}, use_global_device_ids=true, to_apply=%region_13.15 | all-reduce | flops 192 | bytes 1536 | tf_op jit(solution)/shard_map/psum | solution.py:24
  148.7 0.7 cholesky.59
  149.5 0.6 compare_reduce_fusion.2
  150.1 0.6 fusion.29
  150.8 0.6 custom-call.13
  152.4 0.7 cholesky.70
  153.2 0.6 compare_reduce_fusion.1
  153.8 0.6 fusion.30
  154.5 0.6 custom-call.15
  156.3 1.3 collective-permute-start.4
  157.6 3.3 %collective-permute-done.4 = f32[8,3,2,1,128]{4,0,3,2,1:T(8,128)S(1)} collective-permute-done((f32[8,3,2,1,128]{4,0,3,2,1:T(8,128)S(1)}, f32[8,3,2,1,128]{4,0,3,2,1:T(8,128)S(1)}, u32[]{:S(2)}, u32[]{:S(2)}) %collective-permute-start.4) | collective-permute-done | bytes 24608 | tf_op jit(solution)/shard_map/ppermute | solution.py:19
  160.9 3.2 %collective-permute-start.5 = (f32[8,3,1,9,128]{4,0,3,2,1:T(8,128)S(1)}, f32[8,3,1,9,128]{4,0,3,2,1:T(8,128)S(1)}, u32[]{:S(2)}, u32[]{:S(2)}) collective-permute-start(f32[8,3,1,9,128]{4,0,3,2,1:T(8,128)S(1)} %pad_maximum_fusion.2), channel_id=1, source_target_pairs={{1,0},{2,1},{3,2},{5,4},{6,5},{7,6},{9,8},{10,9},{11,10},{13,12},{... | collective-permute-start | bytes 331784 | tf_op jit(solution)/shard_map/ppermute | solution.py:19
  164.2 4.3 %collective-permute-done.5 = f32[8,3,1,9,128]{4,0,3,2,1:T(8,128)S(1)} collective-permute-done((f32[8,3,1,9,128]{4,0,3,2,1:T(8,128)S(1)}, f32[8,3,1,9,128]{4,0,3,2,1:T(8,128)S(1)}, u32[]{:S(2)}, u32[]{:S(2)}) %collective-permute-start.5) | collective-permute-done | bytes 110624 | tf_op jit(solution)/shard_map/ppermute | solution.py:19
  168.6 15.4 %while.27 = (s32[]{:T(128)}, f32[8,3,3,9,128]{4,0,3,2,1:T(8,128)S(1)}, f32[8,3,3,9,128]{4,0,3,2,1:T(8,128)S(1)}, f32[2,8,128]{2,1,0:T(8,128)S(1)}, f32[2,8,128]{...) while((s32[]{:T(128)}, ...), condition=%wide.region_20.24_spmd.clone, body=%wide.region_19.23_spmd.sunk.clone.sunk | while | flops 28531584 | bytes 3733613 | solution.py:122
  184.0 1.9 collective-permute-start.6
  185.9 1.7 collective-permute-done.6
  187.7 3.8 %collective-permute-start.7 = (f32[8,3,2,1,128]{4,0,3,2,1:T(8,128)S(1)}, f32[8,3,2,1,128]{4,0,3,2,1:T(8,128)S(1)}, u32[]{:S(2)}, u32[]{:S(2)}) collective-permute-start(f32[8,3,2,1,128]{4,0,3,2,1:T(8,128)S(1)} %pad_maximum_fusion.3), channel_id=1, source_target_pairs={{0,4},{4,8},{8,12},{12,16},{16,20},{20,24},{24,28},{28,32},{32,36}... | collective-permute-start | bytes 73736 | tf_op jit(solution)/shard_map/ppermute | solution.py:19
  191.9 0.6 collective-permute-done.7
  192.4 0.5 convolution_bitcast_fusion.2
  193.0 10.0 %psum.170 = f32[8,8]{1,0:T(8,128)S(1)} all-reduce(f32[8,8]{1,0:T(8,128)S(1)} %convolution_bitcast_fusion.2), channel_id=1, replica_groups=mesh['tile_0'=4,'tile_1'=16,'tile_2'=2,'layer_0'=2,'layer_1'=2] {'tile_0'}, use_global_device_ids=true, to_apply=%region_21.25 | all-reduce | flops 64 | bytes 512 | tf_op jit(solution)/shard_map/psum | solution.py:24
  203.0 20.2 %psum.171 = f32[8,8]{1,0:T(8,128)S(1)} all-reduce(f32[8,8]{1,0:T(8,128)S(1)} %psum.170), channel_id=1, replica_groups=mesh['tile_0'=4,'tile_1'=16,'tile_2'=2,'layer_0'=2,'layer_1'=2] {'tile_1'}, use_global_device_ids=true, to_apply=%region_22.26 | all-reduce | flops 64 | bytes 512 | tf_op jit(solution)/shard_map/psum | solution.py:24
  223.1 3.8 %psum.172 = f32[8,8]{1,0:T(8,128)S(1)} all-reduce(f32[8,8]{1,0:T(8,128)S(1)} %psum.171), channel_id=1, replica_groups=mesh['tile_0'=4,'tile_1'=16,'tile_2'=2,'layer_0'=2,'layer_1'=2] {'tile_2'}, use_global_device_ids=true, to_apply=%region_23.27 | all-reduce | flops 64 | bytes 512 | tf_op jit(solution)/shard_map/psum | solution.py:24
  226.9 5.3 %psum.173 = f32[8,8]{1,0:T(8,128)S(1)} all-reduce(f32[8,8]{1,0:T(8,128)S(1)} %psum.172), channel_id=1, replica_groups=mesh['tile_0'=4,'tile_1'=16,'tile_2'=2,'layer_0'=2,'layer_1'=2] {'layer_0'}, use_global_device_ids=true, to_apply=%region_24.28 | all-reduce | flops 64 | bytes 512 | tf_op jit(solution)/shard_map/psum | solution.py:24
  232.2 15.2 %psum.174 = f32[8,8]{1,0:T(8,128)S(1)} all-reduce(f32[8,8]{1,0:T(8,128)S(1)} %psum.173), channel_id=1, replica_groups=mesh['tile_0'=4,'tile_1'=16,'tile_2'=2,'layer_0'=2,'layer_1'=2] {'layer_1'}, use_global_device_ids=true, to_apply=%region_25.29 | all-reduce | flops 64 | bytes 512 | tf_op jit(solution)/shard_map/psum | solution.py:24
  247.5 0.7 cholesky.81
  248.3 0.6 compare_reduce_fusion
  248.9 0.6 fusion.31
  249.6 0.6 custom-call.17
  251.3 0.7 copy.39
  252.0 0.7 copy.40
  (486 shorter events, 32.9 us)
Async XLA Ops:
  0.6 2.3 copy-start.3
  1.6 2.0 copy-start.4
  1.6 5.2 %collective-permute-start = (f32[8,3,2,1,128]{4,3,2,1,0:T(1,128)S(1)}, f32[8,3,2,1,128]{4,3,2,1,0:T(1,128)S(1)}, u32[]{:S(2)}, u32[]{:S(2)}) collective-permute-start(f32[8,3,2,1,128]{4,3,2,1,0:T(1,128)S(1)} %slice.346), channel_id=1, source_target_pairs={{4,0},{8,4},{12,8},{16,12},{20,16},{24,20},{28,24},{32,28},{36,32}... | collective-permute-start | bytes 73736 | tf_op jit(solution)/shard_map/ppermute | solution.py:19
  7.0 11.2 %collective-permute-start.1 = (f32[8,3,1,9,128]{4,3,2,1,0:T(8,128)S(1)}, f32[8,3,1,9,128]{4,3,2,1,0:T(8,128)S(1)}, u32[]{:S(2)}, u32[]{:S(2)}) collective-permute-start(f32[8,3,1,9,128]{4,3,2,1,0:T(8,128)S(1)} %slice.492), channel_id=1, source_target_pairs={{1,0},{2,1},{3,2},{5,4},{6,5},{7,6},{9,8},{10,9},{11,10},{13,12},{... | collective-permute-start | bytes 331784 | tf_op jit(solution)/shard_map/ppermute | solution.py:19
  18.2 0.7 copy-start.1
  18.2 0.7 copy-start.2
  34.0 3.7 %collective-permute-start.2 = (f32[8,3,1,9,128]{4,0,3,2,1:T(8,128)S(1)}, f32[8,3,1,9,128]{4,0,3,2,1:T(8,128)S(1)}, u32[]{:S(2)}, u32[]{:S(2)}) collective-permute-start(f32[8,3,1,9,128]{4,0,3,2,1:T(8,128)S(1)} %slice.355), channel_id=1, source_target_pairs={{0,1},{1,2},{2,3},{4,5},{5,6},{6,7},{8,9},{9,10},{10,11},{12,13},{... | collective-permute-start | bytes 331784 | tf_op jit(solution)/shard_map/ppermute | solution.py:19
  37.7 3.6 %copy-start = (f32[8,3,2,8,128]{4,3,2,1,0:T(8,128)S(1)}, f32[8,3,2,8,128]{4,3,2,1,0:T(8,128)}, u32[]{:S(2)}) copy-start(f32[8,3,2,8,128]{4,3,2,1,0:T(8,128)} %param.13) | copy-start | bytes 589828
  37.7 4.5 %collective-permute-start.3 = (f32[8,3,2,1,128]{4,0,3,2,1:T(8,128)S(1)}, f32[8,3,2,1,128]{4,0,3,2,1:T(8,128)S(1)}, u32[]{:S(2)}, u32[]{:S(2)}) collective-permute-start(f32[8,3,2,1,128]{4,0,3,2,1:T(8,128)S(1)} %pad_maximum_fusion.4), channel_id=1, source_target_pairs={{0,4},{4,8},{8,12},{12,16},{16,20},{20,24},{24,28},{28,32},{32,36}... | collective-permute-start | bytes 73736 | tf_op jit(solution)/shard_map/ppermute | solution.py:19
  156.3 4.6 %collective-permute-start.4 = (f32[8,3,2,1,128]{4,0,3,2,1:T(8,128)S(1)}, f32[8,3,2,1,128]{4,0,3,2,1:T(8,128)S(1)}, u32[]{:S(2)}, u32[]{:S(2)}) collective-permute-start(f32[8,3,2,1,128]{4,0,3,2,1:T(8,128)S(1)} %slice.493), channel_id=1, source_target_pairs={{4,0},{8,4},{12,8},{16,12},{20,16},{24,20},{28,24},{32,28},{36,32}... | collective-permute-start | bytes 73736 | tf_op jit(solution)/shard_map/ppermute | solution.py:19
  160.9 7.6 %collective-permute-start.5 = (f32[8,3,1,9,128]{4,0,3,2,1:T(8,128)S(1)}, f32[8,3,1,9,128]{4,0,3,2,1:T(8,128)S(1)}, u32[]{:S(2)}, u32[]{:S(2)}) collective-permute-start(f32[8,3,1,9,128]{4,0,3,2,1:T(8,128)S(1)} %pad_maximum_fusion.2), channel_id=1, source_target_pairs={{1,0},{2,1},{3,2},{5,4},{6,5},{7,6},{9,8},{10,9},{11,10},{13,12},{... | collective-permute-start | bytes 331784 | tf_op jit(solution)/shard_map/ppermute | solution.py:19
  184.0 3.7 %collective-permute-start.6 = (f32[8,3,1,9,128]{4,0,3,2,1:T(8,128)S(1)}, f32[8,3,1,9,128]{4,0,3,2,1:T(8,128)S(1)}, u32[]{:S(2)}, u32[]{:S(2)}) collective-permute-start(f32[8,3,1,9,128]{4,0,3,2,1:T(8,128)S(1)} %slice.363), channel_id=1, source_target_pairs={{0,1},{1,2},{2,3},{4,5},{5,6},{6,7},{8,9},{9,10},{10,11},{12,13},{... | collective-permute-start | bytes 331784 | tf_op jit(solution)/shard_map/ppermute | solution.py:19
  187.7 4.8 %collective-permute-start.7 = (f32[8,3,2,1,128]{4,0,3,2,1:T(8,128)S(1)}, f32[8,3,2,1,128]{4,0,3,2,1:T(8,128)S(1)}, u32[]{:S(2)}, u32[]{:S(2)}) collective-permute-start(f32[8,3,2,1,128]{4,0,3,2,1:T(8,128)S(1)} %pad_maximum_fusion.3), channel_id=1, source_target_pairs={{0,4},{4,8},{8,12},{12,16},{16,20},{20,24},{24,28},{28,32},{32,36}... | collective-permute-start | bytes 73736 | tf_op jit(solution)/shard_map/ppermute | solution.py:19
where the time goes:
time: 253 us
  blocking collectives  160 us (63%)
  starting transfers between devices  26.3 us (10%)
  local copies, waits for them, and re-layouts  21.2 us (8%)
  matrix products  15.2 us (6%)
  other arithmetic  13.7 us (5%)
  waiting for transfers between devices  12.3 us (5%)
  loops' own time  3.37 us (1%)
    psum x10, blocking collectives, one_axis_at_a_time(): array = lax.psum(array, axis)  160 us
    ppermute x8, starting transfers between devices, from_behind(): return lax.ppermute(array, axis, pairs)  26.3 us
    ppermute x8, waiting for transfers between devices, from_behind(): return lax.ppermute(array, axis, pairs)  12.3 us
    dot_general x32, matrix products, element_forces(): jnp.dot(tables, scaled, precision=lax.Precision.HIGHEST, preferred_elemen...  9.75 us
    concatenate x16, local copies, waits for them, and re-layouts, element_forces(): stacked = jnp.concatenate(pieces, 0)  6.37 us
  transfers between devices with their start and end apart: 8, of which 7 were waited for; matrix products, arithmetic and copies ran while one was open for 3% of the time, Pallas kernels for 0%

commit v1 on v0

v1 whole, which is shorter than its diff:
```python
import jax
import jax.numpy as jnp
from jax import lax
from jax.experimental import pallas as pl
from jax.experimental.pallas import tpu as pltpu
from jax.sharding import Mesh
from jax.sharding import PartitionSpec as P

TILE = ("tile_0", "tile_1", "tile_2")
LAYER = ("layer_0", "layer_1")
PLANE = ("tile_0", "tile_2", "layer_0", "layer_1")
COLUMN = "tile_1"

PROBES = 8
OWN_Z = 2
OWN_X = 8
WIDE_X = OWN_X + 4
WIDE_Z = OWN_Z + 4
SPAN = 128
ROWS = 3 * OWN_Z * OWN_X
EDGE = 13
FULL = 6 * WIDE_X + 6
F32 = jnp.float32
HIGHEST = lax.Precision.HIGHEST


def vregs(*shape):
    return jax.ShapeDtypeStruct((*shape, 8, SPAN), F32)


def call(kernel, out_shape, scratch=(), smem=()):
    def run(*args):
        specs = [
            pl.BlockSpec(memory_space=pltpu.SMEM if i in smem else pltpu.VMEM)
            for i in range(len(args))
        ]
        outs = out_shape if isinstance(out_shape, (list, tuple)) else None
        out_specs = (
            [pl.BlockSpec(memory_space=pltpu.VMEM)] * len(outs)
            if outs
            else pl.BlockSpec(memory_space=pltpu.VMEM)
        )
        return pl.pallas_call(
            kernel,
            out_shape=out_shape,
            in_specs=specs,
            out_specs=out_specs,
            scratch_shapes=list(scratch),
            name=kernel.__name__,
        )(*args)

    return run


def pack_kernel(lame, probes, material, own, to_y, to_z):
    odd = lax.axis_index("tile_2") == 1
    for z in range(OWN_Z):
        for x in range(OWN_X):
            for c in range(3):
                own[(z * OWN_X + x) * 3 + c] = probes[
                    pl.ds((c * OWN_Z + z) * OWN_X + x, PROBES, stride=ROWS), :
                ]
    fields = {}
    for z in range(OWN_Z):
        kinds = material[z]
        for k in range(2):
            value = jnp.where(
                kinds == 0, lame[0, k], jnp.where(kinds == 1, lame[1, k], lame[2, k])
            )
            fields[k, z] = value * (1.0 / 16.0)
            own[48 + k * 2 + z] = fields[k, z]
    first_y = jnp.where(odd, 0, OWN_X - 2)
    first_z = jnp.where(odd, OWN_X - 2, 0)
    for first, to in ((first_y, to_y), (first_z, to_z)):
        for z in range(OWN_Z):
            for xx in range(2):
                for c in range(3):
                    to[(z * 2 + xx) * 3 + c] = own[(z * OWN_X + first + xx) * 3 + c]
    low = jnp.concatenate([fields[k, z][0:2] for k in range(2) for z in range(2)], 0)
    high = jnp.concatenate([fields[k, z][6:8] for k in range(2) for z in range(2)], 0)
    to_y[12] = jnp.where(odd, low, high)
    to_z[12] = jnp.where(odd, high, low)


def widen_kernel(own, from_y, from_z, full):
    odd = lax.axis_index("tile_2") == 1
    for z in range(OWN_Z):
        for c in range(3):
            for x in range(OWN_X):
                full[(z * WIDE_X + 2 + x) * 3 + c] = own[(z * OWN_X + x) * 3 + c]
            for xx in range(2):
                at = (z * 2 + xx) * 3 + c
                full[(z * WIDE_X + xx) * 3 + c] = jnp.where(odd, from_y[at], from_z[at])
                full[(z * WIDE_X + 10 + xx) * 3 + c] = jnp.where(odd, from_z[at], from_y[at])
    for i in range(4):
        full[72 + i] = own[48 + i]
    full[76] = jnp.where(odd, from_y[12], from_z[12])
    full[77] = jnp.where(odd, from_z[12], from_y[12])


def stress(modes, lam, mu):
    a, b, e, p, q, r, t = modes
    third = 1.0 / 3.0
    lam3 = lam * third
    mu3 = mu * third
    both = mu + lam3
    top = (4.0 * mu + lam) * (1.0 / 9.0)
    twice = mu + mu
    trace = lam * (a[0] + b[1] + e[2])
    s01 = mu * (b[0] + a[1])
    s02 = mu * (e[0] + a[2])
    s12 = mu * (e[1] + b[2])
    aa = (twice * a[0] + trace, s01, s02)
    bb = (s01, twice * b[1] + trace, s12)
    ee = (s02, s12, twice * e[2] + trace)
    mixed = p[2] + q[1] + r[0]
    pp = (both * p[0] + lam3 * r[2], both * p[1] + lam3 * q[2], mu3 * (p[2] + mixed))
    qq = (both * q[0] + lam3 * r[1], mu3 * (q[1] + mixed), both * q[2] + lam3 * p[1])
    rr = (mu3 * (r[0] + mixed), both * r[1] + lam3 * q[0], both * r[2] + lam3 * p[0])
    tt = tuple(top * t[c] for c in range(3))
    return aa, bb, ee, pp, qq, rr, tt


def element_column(load, fields, height, emit):
    def along_x(z):
        values = []
        for c in range(3):
            s0, d0, s1, d1 = load(z, c)
            values.append((s0 + s1, s1 - s0, d0 + d1, d1 - d0))
        return values

    below = along_x(0)
    carried = None
    for z in range(height):
        above = along_x(z + 1)
        modes = tuple(
            tuple(
                above[c][kind] - below[c][kind] if minus else above[c][kind] + below[c][kind]
                for c in range(3)
            )
            for kind, minus in (
                (0, True),
                (1, False),
                (2, False),
                (1, True),
                (2, True),
                (3, False),
                (3, True),
            )
        )
        lam, mu = fields(z)
        aa, bb, ee, pp, qq, rr, tt = stress(modes, lam, mu)
        if carried is not None:
            emit(
                z,
                [
                    (
                        carried[c][0] - aa[c],
                        carried[c][1] + (bb[c] - pp[c]),
                        carried[c][2] + (ee[c] - qq[c]),
                        carried[c][3] + (rr[c] - tt[c]),
                    )
                    for c in range(3)
                ],
            )
        carried = [(aa[c], bb[c] + pp[c], ee[c] + qq[c], rr[c] + tt[c]) for c in range(3)]
        below = above


def stencil_kernel(full, from_a, from_b, block, message, pair, pair_one, lams, mus, carry):
    core = lax.axis_index("layer_1")
    layer = lax.axis_index("layer_0") * 2 + core
    tile = (lax.axis_index("tile_0") * 16 + lax.axis_index("tile_1")) * 2 + lax.axis_index("tile_2")
    lanes = lax.broadcasted_iota(jnp.int32, (8, SPAN), 1)
    not_last = jnp.where(lanes == SPAN - 1, 0.0, 1.0).astype(F32)
    not_first = jnp.where(lanes == 0, 0.0, 1.0).astype(F32)
    keep_z = jnp.where(layer == 3, 0.0, 1.0).astype(F32)
    keep_x = jnp.where(tile == 127, 0.0, 1.0).astype(F32)

    def spread(value):
        after = pltpu.roll(value, SPAN - 1, 1) * not_last
        return value + after, after - value

    offset_a = jnp.where(core == 0, 4, 0)
    offset_b = jnp.where(core == 0, 0, 4)
    for source, offset in ((full, 2), (from_a, offset_a), (from_b, offset_b)):

        def fill(x, _, source=source, offset=offset):
            for z in range(OWN_Z):
                for c in range(3):
                    value = source[(z * WIDE_X + x) * 3 + c]
                    at = (((offset + z) * WIDE_X + x) * 3 + c) * 2
                    both = spread(value)
                    pair[at] = both[0]
                    pair[at + 1] = both[1]
            return 0

        lax.fori_loop(0, WIDE_X, fill, 0)
        for k, target in ((0, lams), (1, mus)):
            for z in range(OWN_Z):
                for x in range(WIDE_X):
                    if x < 2:
                        row = source[76, k * 4 + z * 2 + x : k * 4 + z * 2 + x + 1, :]
                    elif x < 10:
                        row = source[72 + k * 2 + z, x - 2 : x - 1, :]
                    else:
                        row = source[77, k * 4 + z * 2 + x - 10 : k * 4 + z * 2 + x - 9, :]
                    target[(offset + z) * WIDE_X + x] = jnp.broadcast_to(row, (8, SPAN))
    for x in range(OWN_X):
        for z in range(OWN_Z):
            for c in range(3):
                at = ((x + 2) * 6 + z * 3 + c) * SPAN
                block[0:8, at : at + SPAN] = full[(z * WIDE_X + 2 + x) * 3 + c]

    def finish(x, z, c, slot, parts):
        ss, ds, sd, dd = parts
        total_s = carry[slot] + (ss - ds)
        total_d = carry[slot + 1] + (sd - dd)
        carry[slot] = ss + ds
        carry[slot + 1] = sd + dd
        return (total_s - total_d) + pltpu.roll(total_s + total_d, 1, 1) * not_first

    carry[...] = jnp.zeros(carry.shape, F32)

    def first(x, _):
        def load(z, c):
            at = ((z * WIDE_X + x) * 3 + c) * 2
            return pair[at], pair[at + 1], pair[at + 6], pair[at + 7]

        def fields(z):
            return lams[z * WIDE_X + x], mus[z * WIDE_X + x]

        inside = jnp.where(x == 10, keep_x, 1.0)

        def emit(z, forces):
            keep = inside * keep_z if z == 4 else inside
            for c in range(3):
                value = finish(x, z, c, ((z - 1) * 3 + c) * 2, forces[c]) * keep
                if z in (2, 3):
                    at = pl.multiple_of((x * 6 + (z - 2) * 3 + c) * SPAN, SPAN)
                    block[8:16, pl.ds(at, SPAN)] = value
                both = spread(value)
                at = (((z - 1) * WIDE_X + x) * 3 + c) * 2
                pair_one[at] = both[0]
                pair_one[at + 1] = both[1]

        element_column(load, fields, 5, emit)
        return 0

    lax.fori_loop(0, WIDE_X - 1, first, 0)
    carry[...] = jnp.zeros(carry.shape, F32)

    def second(x, _):
        def load(z, c):
            at = ((z * WIDE_X + x) * 3 + c) * 2
            return pair_one[at], pair_one[at + 1], pair_one[at + 6], pair_one[at + 7]

        def fields(z):
            return lams[(z + 1) * WIDE_X + x], mus[(z + 1) * WIDE_X + x]

        def emit(z, forces):
            for c in range(3):
                value = finish(x, z, c, ((z - 1) * 3 + c) * 2, forces[c])
                at = pl.multiple_of((x * 6 + (z - 1) * 3 + c) * SPAN, SPAN)
                block[16:24, pl.ds(at, SPAN)] = value

        element_column(load, fields, 3, emit)
        return 0

    lax.fori_loop(1, WIDE_X - 2, second, 0)
    every = block[:, 12 * SPAN : 60 * SPAN]
    grams = lax.dot_general(
        every[0:16], every, (((1,), (1,)), ((), ())), precision=HIGHEST, preferred_element_type=F32
    )
    wide = jnp.concatenate([grams, jnp.zeros((16, SPAN - 24), F32)], 1)
    packed = jnp.where(lanes < 16, wide[0:8], pltpu.roll(wide[8:16], 8, 1))
    for i in range(message.shape[0]):
        message[i] = packed


def total_kernel(parts, message):
    total = parts[0]
    for i in range(1, parts.shape[0]):
        total = total + parts[i]
    for i in range(message.shape[0]):
        message[i] = total


def eliminate(table, first):
    rows = lax.broadcasted_iota(jnp.int32, (8, SPAN), 0)
    for k in range(8):
        pivot_row = jnp.broadcast_to(table[k : k + 1, :], (8, SPAN))
        column = jnp.broadcast_to(table[:, first + k : first + k + 1], (8, SPAN))
        pivot = jnp.broadcast_to(table[k : k + 1, first + k : first + k + 1], (8, SPAN))
        scaled = pivot_row / pivot
        table = jnp.where(rows == k, scaled, table - column * scaled)
    return table


def times(left, first, right):
    total = None
    for k in range(8):
        column = jnp.broadcast_to(left[:, first + k : first + k + 1], (8, SPAN))
        row = jnp.broadcast_to(right[k : k + 1, :], (8, SPAN))
        total = column * row if total is None else total + column * row
    return total


def final_kernel(parts, block, solution_rows, residual_rows):
    table = parts[0]
    for i in range(1, parts.shape[0]):
        table = table + parts[i]
    lanes = lax.broadcasted_iota(jnp.int32, (8, SPAN), 1)
    solved = eliminate(table, 8)
    product = times(table, 16, solved)
    shifted = pltpu.roll(table, SPAN - 8, 1)
    second = jnp.where(lanes < 8, product - shifted, shifted - product)
    coef_c = jnp.where(lanes < 8, eliminate(second, 16), 0.0)
    coef_b = jnp.where(lanes < 8, solved + times(solved, 16, coef_c), 0.0)
    coefs = jnp.concatenate(
        [coef_b, -coef_c - pltpu.roll(coef_b, 8, 1), pltpu.roll(coef_c, 8, 1)], 0
    )[:, 0:16]
    every = block[:, 12 * SPAN : 60 * SPAN]
    mixed = lax.dot_general(
        coefs, every, (((0,), (0,)), ((), ())), precision=HIGHEST, preferred_element_type=F32
    )
    for x in range(OWN_X):
        for z in range(OWN_Z):
            for c in range(3):
                at = (x * 6 + z * 3 + c) * SPAN
                row = (c * OWN_Z + z) * OWN_X + x
                solution_rows[pl.ds(row, PROBES, stride=ROWS), :] = mixed[0:8, at : at + SPAN]
                residual_rows[pl.ds(row, PROBES, stride=ROWS), :] = (
                    every[0:8, at : at + SPAN] + mixed[8:16, at : at + SPAN]
                )


def body(probes, material, lame_pairs):
    tiles = lax.axis_size(TILE)
    in_y = [(i, i ^ 1) for i in range(tiles)]
    in_z = [(i, ((i + 1) ^ 1) - 1) for i in range(1, tiles - 1)]
    in_core = [(0, 1), (1, 0), (2, 3), (3, 2)]
    in_chip = [(1, 2), (2, 1)]
    own, to_y, to_z = call(pack_kernel, (vregs(52), vregs(EDGE), vregs(EDGE)), smem=(0,))(
        lame_pairs, probes.reshape(PROBES * ROWS, SPAN), material
    )
    from_z = lax.ppermute(to_z, TILE, in_z)
    from_y = lax.ppermute(to_y, TILE, in_y)
    full = call(widen_kernel, vregs(FULL))(own, from_y, from_z)
    from_b = lax.ppermute(full, LAYER, in_chip)
    from_a = lax.ppermute(full, LAYER, in_core)
    planes = lax.axis_size(PLANE)
    columns = lax.axis_size(COLUMN)
    block, message = call(
        stencil_kernel,
        (jax.ShapeDtypeStruct((24, 6 * WIDE_X * SPAN), F32), vregs(planes)),
        scratch=(
            pltpu.VMEM((WIDE_Z * WIDE_X * 6, 8, SPAN), F32),
            pltpu.VMEM(((OWN_Z + 2) * WIDE_X * 6, 8, SPAN), F32),
            pltpu.VMEM((WIDE_Z * WIDE_X, 8, SPAN), F32),
            pltpu.VMEM((WIDE_Z * WIDE_X, 8, SPAN), F32),
            pltpu.VMEM((24, 8, SPAN), F32),
        ),
    )(full, from_a, from_b)
    parts = lax.all_to_all(message, PLANE, 0, 0, tiled=True)
    message = call(total_kernel, vregs(columns))(parts)
    parts = lax.all_to_all(message, COLUMN, 0, 0, tiled=True)
    rows = jax.ShapeDtypeStruct((PROBES * ROWS, SPAN), F32)
    solution_rows, residual_rows = call(final_kernel, (rows, rows))(parts, block)
    return solution_rows.reshape(probes.shape), residual_rows.reshape(probes.shape)


def solution(mesh):
    split = Mesh(
        mesh.devices.reshape(4, 16, 2, 2, 2), ("tile_0", "tile_1", "tile_2", "layer_0", "layer_1")
    )
    spread = P(None, None, LAYER, TILE, None)
    return jax.shard_map(
        body,
        mesh=split,
        in_specs=(spread, P(LAYER, TILE, None), P()),
        out_specs=(spread, spread),
        check_vma=False,
    )
```

time: 253 us -> 87.3 us (0.35)
  blocking collectives: 160 us -> 47 us
  Pallas kernels: 0 us -> 18.5 us
  local copies, waits for them, and re-layouts: 21.2 us -> 3.41 us
  matrix products: 15.2 us -> 0 us
  other arithmetic: 13.7 us -> 0 us
  starting transfers between devices: 26.3 us -> 14.6 us
  waiting for transfers between devices: 12.3 us -> 2.68 us
  loops' own time: 3.37 us -> 0 us
    psum x10 -> x0, blocking collectives: 160 us -> none  [one_axis_at_a_time(): array = lax.psum(array, axis)]
    all_to_all x0 -> x2, blocking collectives: none -> 47 us  [the longest x1 26.1 us: body(): parts = lax.all_to_all(message, PLANE, 0, 0, tiled=True)]
    pallas_call x0 -> x5, Pallas kernels: none -> 18.5 us  [run(): pl.pallas_call(kernel, out_shape=out_shape, in_specs=specs, out_specs=out...]
    dot_general x44 -> x0, matrix products: 14.1 us -> none  [the longest x32 9.75 us: element_forces(): jnp.dot(tables, scaled, precision=lax.Precision.HIGHEST, preferred_elemen...]
    ppermute x8 -> x4, starting transfers between devices: 26.3 us -> 14.6 us  [the longest x1 6.68 us: body(): from_b = lax.ppermute(full, LAYER, in_chip)]
    ppermute x8 -> x4, waiting for transfers between devices: 12.3 us -> 2.68 us  [the longest x1 1.63 us: body(): from_b = lax.ppermute(full, LAYER, in_chip)]
    another operation x15 -> x0, other arithmetic: 8.01 us -> none  [the longest x9 4.19 us: spd_solve(): lower_factor = jnp.linalg.cholesky(matrix)]
    concatenate x17 -> x0, local copies, waits for them, and re-layouts: 6.48 us -> none  [the longest x16 6.37 us: element_forces(): stacked = jnp.concatenate(pieces, 0)]
  transfers between devices with their start and end apart: 8 -> 4, of which waited for: 7 -> 2; matrix products, arithmetic and copies ran while one was open for 3% -> 0% of each run, Pallas kernels for 0% -> 0%
where the time goes in v1:
time: 87.3 us; the launch traced here: 86.8 us
  blocking collectives  47 us (54%)
  Pallas kernels  18.5 us (21%)
  starting transfers between devices  14.6 us (17%)
  local copies, waits for them, and re-layouts  3.41 us (4%)
  waiting for transfers between devices  2.68 us (3%)
    all_to_all x1, blocking collectives, body(): parts = lax.all_to_all(message, PLANE, 0, 0, tiled=True)  26.1 us
    all_to_all x1, blocking collectives, body(): parts = lax.all_to_all(message, COLUMN, 0, 0, tiled=True)  20.9 us
    pallas_call x5, Pallas kernels, run(): pl.pallas_call(kernel, out_shape=out_shape, in_specs=specs, out_specs=out...  18.5 us
    ppermute x1, starting transfers between devices, body(): from_b = lax.ppermute(full, LAYER, in_chip)  6.68 us
    ppermute x1, starting transfers between devices, body(): from_y = lax.ppermute(to_y, TILE, in_y)  4.01 us
    unnamed x9, local copies, waits for them, and re-layouts  3.41 us
    ppermute x1, starting transfers between devices, body(): from_a = lax.ppermute(full, LAYER, in_core)  3.23 us
  transfers between devices with their start and end apart: 4, of which 2 were waited for; matrix products, arithmetic and copies ran while one was open for 0% of the time, Pallas kernels for 0%

profile of v1, /device:TPU:1, one launch (start us, length us, event | category | flops | bytes accessed | tf_op | source)
XLA Modules:
  0.0 86.8 jit_solution(1745088506875149809)
XLA Ops:
  0.6 1.3 %copy.5.lame = f32[3,2]{1,0:T(4,128)} copy(f32[3,2]{0,1:T(2,128)} %param.5) | data formatting | bytes 48 | tf_op args[2]
  2.0 1.7 %pack_kernel.1 = (f32[52,8,128]{2,1,0:T(8,128)}, f32[13,8,128]{2,1,0:T(8,128)}, f32[13,8,128]{2,1,0:T(8,128)}) custom-call(f32[3,2]{1,0:T(4,128)} %copy.5.lame, f32[384,128]{1,0:T(8,128)} %bitcast.3, s32[2,8,128]{2,1,0:T(8,128)} %material.1), custom_call_target="tpu_custom_call" | custom-call | tf_op jit(solution)/shard_map/pack_kernel/pallas_call | solution.py:43
  3.7 4.0 %collective-permute-start = (f32[13,8,128]{2,1,0:T(8,128)}, f32[13,8,128]{2,1,0:T(8,128)S(1)}, u32[]{:S(2)}, u32[]{:S(2)}) collective-permute-start(f32[13,8,128]{2,1,0:T(8,128)} %get-tuple-element.10), channel_id=1, source_target_pairs={{0,4},{4,0},{8,12},{12,8},{16,20},{20,16},{24,28},{28,24},{32,36},... | collective-permute-start | bytes 159752 | tf_op jit(solution)/shard_map/ppermute | solution.py:348
  7.7 0.7 collective-permute-start.1
  8.4 1.0 %collective-permute-done.from_y = f32[13,8,128]{2,1,0:T(8,128)S(1)} collective-permute-done((f32[13,8,128]{2,1,0:T(8,128)}, f32[13,8,128]{2,1,0:T(8,128)S(1)}, u32[]{:S(2)}, u32[]{:S(2)}) %collective-permute-start) | collective-permute-done | bytes 53280 | tf_op jit(solution)/shard_map/ppermute | solution.py:348
  9.4 0.0 copy-start.2
  9.4 0.0 collective-permute-done.1.from_z
  9.4 0.0 copy-start.3
  9.4 0.6 copy-done.2
  10.0 0.0 copy-done.3
  10.1 1.7 %widen_kernel.1.full = f32[78,8,128]{2,1,0:T(8,128)} custom-call(f32[52,8,128]{2,1,0:T(8,128)} %get-tuple-element.9.own, f32[13,8,128]{2,1,0:T(8,128)} %copy-done.2, f32[13,8,128]{2,1,0:T(8,128)} %copy-done.3), custom_call_target="tpu_custom_call" | custom-call | tf_op jit(solution)/shard_map/widen_kernel/pallas_call | solution.py:43
  11.8 6.7 %collective-permute-start.3 = (f32[78,8,128]{2,1,0:T(8,128)}, f32[78,8,128]{2,1,0:T(8,128)S(1)}, u32[]{:S(2)}, u32[]{:S(2)}) collective-permute-start(f32[78,8,128]{2,1,0:T(8,128)} %widen_kernel.1.full), channel_id=1, source_target_pairs={{1,2},{2,1},{5,6},{6,5},{9,10},{10,9},{13,14},{14,13},{17,18},{18,... | collective-permute-start | bytes 958472 | tf_op jit(solution)/shard_map/ppermute | solution.py:350
  18.5 3.2 %collective-permute-start.2 = (f32[78,8,128]{2,1,0:T(8,128)}, f32[78,8,128]{2,1,0:T(8,128)S(1)}, u32[]{:S(2)}, u32[]{:S(2)}) collective-permute-start(f32[78,8,128]{2,1,0:T(8,128)} %widen_kernel.1.full), channel_id=1, source_target_pairs={{0,1},{1,0},{2,3},{3,2},{4,5},{5,4},{6,7},{7,6},{8,9},{9,8},{10,11... | collective-permute-start | bytes 958472 | tf_op jit(solution)/shard_map/ppermute | solution.py:351
  21.7 1.6 %collective-permute-done.3.from_b = f32[78,8,128]{2,1,0:T(8,128)S(1)} collective-permute-done((f32[78,8,128]{2,1,0:T(8,128)}, f32[78,8,128]{2,1,0:T(8,128)S(1)}, u32[]{:S(2)}, u32[]{:S(2)}) %collective-permute-start.3) | collective-permute-done | bytes 319520 | tf_op jit(solution)/shard_map/ppermute | solution.py:350
  23.3 0.0 copy-start
  23.3 0.0 collective-permute-done.2.from_a
  23.3 0.7 copy-done
  24.1 0.0 copy-start.1
  24.1 0.7 copy-done.1
  24.8 9.0 %stencil_kernel.1 = (f32[24,9216]{1,0:T(8,128)}, f32[32,8,128]{2,1,0:T(8,128)}) custom-call(f32[78,8,128]{2,1,0:T(8,128)} %widen_kernel.1.full, f32[78,8,128]{2,1,0:T(8,128)} %copy-done.1, f32[78,8,128]{2,1,0:T(8,128)} %copy-done), custom_call_target="tpu_custom_call" | custom-call | tf_op jit(solution)/shard_map/stencil_kernel/pallas_call | solution.py:43
  33.8 26.1 %all_to_all.10.parts = f32[32,8,128]{2,1,0:T(8,128)} all-to-all(f32[32,8,128]{2,1,0:T(8,128)} %get-tuple-element.12), channel_id=1, replica_groups=mesh['tile_0'=4,'tile_1'=16,'tile_2'=2,'layer_0'=2,'layer_1'=2] {'tile_0..., dimensions={0} | all-to-all | bytes 262144 | tf_op jit(solution)/shard_map/all_to_all | solution.py:365
  59.9 1.6 %total_kernel.1 = f32[16,8,128]{2,1,0:T(8,128)} custom-call(f32[32,8,128]{2,1,0:T(8,128)} %all_to_all.10.parts), custom_call_target="tpu_custom_call" | custom-call | tf_op jit(solution)/shard_map/total_kernel/pallas_call | solution.py:43
  61.4 20.9 %all_to_all.11.parts = f32[16,8,128]{2,1,0:T(8,128)} all-to-all(f32[16,8,128]{2,1,0:T(8,128)} %total_kernel.1), channel_id=1, replica_groups=mesh['tile_0'=4,'tile_1'=16,'tile_2'=2,'layer_0'=2,'layer_1'=2] {'tile_1'}, dimensions={0} | all-to-all | bytes 131072 | tf_op jit(solution)/shard_map/all_to_all | solution.py:367
  82.3 4.5 %final_kernel.1 = (f32[384,128]{1,0:T(8,128)}, f32[384,128]{1,0:T(8,128)}) custom-call(f32[16,8,128]{2,1,0:T(8,128)} %all_to_all.11.parts, f32[24,9216]{1,0:T(8,128)} %get-tuple-element.13.block), custom_call_target="tpu_custom_call" | custom-call | tf_op jit(solution)/shard_map/final_kernel/pallas_call | solution.py:43
Async XLA Ops:
  3.7 5.7 %collective-permute-start = (f32[13,8,128]{2,1,0:T(8,128)}, f32[13,8,128]{2,1,0:T(8,128)S(1)}, u32[]{:S(2)}, u32[]{:S(2)}) collective-permute-start(f32[13,8,128]{2,1,0:T(8,128)} %get-tuple-element.10), channel_id=1, source_target_pairs={{0,4},{4,0},{8,12},{12,8},{16,20},{20,16},{24,28},{28,24},{32,36},... | collective-permute-start | bytes 159752 | tf_op jit(solution)/shard_map/ppermute | solution.py:348
  7.7 1.7 %collective-permute-start.1 = (f32[13,8,128]{2,1,0:T(8,128)}, f32[13,8,128]{2,1,0:T(8,128)S(1)}, u32[]{:S(2)}, u32[]{:S(2)}) collective-permute-start(f32[13,8,128]{2,1,0:T(8,128)} %get-tuple-element.11), channel_id=1, source_target_pairs={{4,8},{8,4},{12,16},{16,12},{20,24},{24,20},{28,32},{32,28},{36,40... | collective-permute-start | bytes 159752 | tf_op jit(solution)/shard_map/ppermute | solution.py:347
  9.4 0.6 copy-start.2
  9.4 0.6 copy-start.3
  11.8 11.6 %collective-permute-start.3 = (f32[78,8,128]{2,1,0:T(8,128)}, f32[78,8,128]{2,1,0:T(8,128)S(1)}, u32[]{:S(2)}, u32[]{:S(2)}) collective-permute-start(f32[78,8,128]{2,1,0:T(8,128)} %widen_kernel.1.full), channel_id=1, source_target_pairs={{1,2},{2,1},{5,6},{6,5},{9,10},{10,9},{13,14},{14,13},{17,18},{18,... | collective-permute-start | bytes 958472 | tf_op jit(solution)/shard_map/ppermute | solution.py:350
  18.5 4.9 %collective-permute-start.2 = (f32[78,8,128]{2,1,0:T(8,128)}, f32[78,8,128]{2,1,0:T(8,128)S(1)}, u32[]{:S(2)}, u32[]{:S(2)}) collective-permute-start(f32[78,8,128]{2,1,0:T(8,128)} %widen_kernel.1.full), channel_id=1, source_target_pairs={{0,1},{1,0},{2,3},{3,2},{4,5},{5,4},{6,7},{7,6},{8,9},{9,8},{10,11... | collective-permute-start | bytes 958472 | tf_op jit(solution)/shard_map/ppermute | solution.py:351
  23.3 0.7 copy-start
  24.1 0.7 copy-start.1

commit v2 on v1

--- a/solution.py
+++ b/solution.py
@@ -25,14 +25,20 @@
 
 
 def vregs(*shape):
-    return jax.ShapeDtypeStruct((*shape, 8, SPAN), F32)
-
-
-def call(kernel, out_shape, scratch=(), smem=()):
+    return pltpu.VMEM((*shape, 8, SPAN), F32)
+
+
+def call(kernel, out_shape, scratch=(), smem=(), outside=()):
     def run(*args):
         specs = [
             pl.BlockSpec(memory_space=pltpu.SMEM if i in smem else pltpu.VMEM)
             for i in range(len(args))
+        ]
+        args = [
+            arg
+            if i in smem or i in outside
+            else pltpu.with_memory_space_constraint(arg, pltpu.VMEM)
+            for i, arg in enumerate(args)
         ]
         outs = out_shape if isinstance(out_shape, (list, tuple)) else None
         out_specs = (
@@ -65,7 +71,7 @@
         kinds = material[z]
         for k in range(2):
             value = jnp.where(
-                kinds == 0, lame[0, k], jnp.where(kinds == 1, lame[1, k], lame[2, k])
+                kinds == 0, lame[k, 0], jnp.where(kinds == 1, lame[k, 1], lame[k, 2])
             )
             fields[k, z] = value * (1.0 / 16.0)
             own[48 + k * 2 + z] = fields[k, z]
@@ -341,8 +347,8 @@
     in_z = [(i, ((i + 1) ^ 1) - 1) for i in range(1, tiles - 1)]
     in_core = [(0, 1), (1, 0), (2, 3), (3, 2)]
     in_chip = [(1, 2), (2, 1)]
-    own, to_y, to_z = call(pack_kernel, (vregs(52), vregs(EDGE), vregs(EDGE)), smem=(0,))(
-        lame_pairs, probes.reshape(PROBES * ROWS, SPAN), material
+    own, to_y, to_z = call(pack_kernel, (vregs(52), vregs(EDGE), vregs(EDGE)), smem=(0,), outside=(1, 2))(
+        lame_pairs.T, probes.reshape(PROBES * ROWS, SPAN), material
     )
     from_z = lax.ppermute(to_z, TILE, in_z)
     from_y = lax.ppermute(to_y, TILE, in_y)
@@ -353,7 +359,7 @@
     columns = lax.axis_size(COLUMN)
     block, message = call(
         stencil_kernel,
-        (jax.ShapeDtypeStruct((24, 6 * WIDE_X * SPAN), F32), vregs(planes)),
+        (pltpu.VMEM((24, 6 * WIDE_X * SPAN), F32), vregs(planes)),
         scratch=(
             pltpu.VMEM((WIDE_Z * WIDE_X * 6, 8, SPAN), F32),
             pltpu.VMEM(((OWN_Z + 2) * WIDE_X * 6, 8, SPAN), F32),

time: 87.3 us -> 75.9 us (0.87)
  Pallas kernels: 18.5 us -> 11.7 us
  local copies, waits for them, and re-layouts: 3.41 us -> 0 us
    pallas_call x5, Pallas kernels: 18.5 us -> 11.7 us  [run(): pl.pallas_call(kernel, out_shape=out_shape, in_specs=specs, out_specs=out...]
    unnamed x9 -> x0, local copies, waits for them, and re-layouts: 3.41 us -> none
where the time goes in v2:
time: 75.9 us; the launch traced here: 75.6 us
  blocking collectives  46.4 us (61%)
  starting transfers between devices  14.6 us (19%)
  Pallas kernels  11.7 us (15%)
  waiting for transfers between devices  2.26 us (3%)
    all_to_all x1, blocking collectives, body(): parts = lax.all_to_all(message, PLANE, 0, 0, tiled=True)  25.8 us
    all_to_all x1, blocking collectives, body(): parts = lax.all_to_all(message, COLUMN, 0, 0, tiled=True)  20.6 us
    pallas_call x5, Pallas kernels, run(): pl.pallas_call(kernel, out_shape=out_shape, in_specs=specs, out_specs=out...  11.7 us
    ppermute x1, starting transfers between devices, body(): from_b = lax.ppermute(full, LAYER, in_chip)  6.69 us
    ppermute x1, starting transfers between devices, body(): from_y = lax.ppermute(to_y, TILE, in_y)  4.02 us
    ppermute x1, starting transfers between devices, body(): from_a = lax.ppermute(full, LAYER, in_core)  3.23 us
  transfers between devices with their start and end apart: 4, of which 2 were waited for; matrix products, arithmetic and copies ran while one was open for 0% of the time, Pallas kernels for 0%

profile of v2, /device:TPU:1, one launch (start us, length us, event | category | flops | bytes accessed | tf_op | source)
XLA Modules:
  0.0 75.6 jit_solution(880755589822866080)
XLA Ops:
  0.6 1.0 %pack_kernel.1 = (f32[52,8,128]{2,1,0:T(8,128)S(1)}, f32[13,8,128]{2,1,0:T(8,128)S(1)}, f32[13,8,128]{2,1,0:T(8,128)S(1)}) custom-call(f32[2,3]{1,0:T(2,128)} %bitcast.5, f32[384,128]{1,0:T(8,128)} %bitcast.4, s32[2,8,128]{2,1,0:T(8,128)} %material.1), custom_call_target="tpu_custom_call" | custom-call | tf_op jit(solution)/shard_map/pack_kernel/pallas_call | solution.py:49
  1.7 4.0 %collective-permute-start = (f32[13,8,128]{2,1,0:T(8,128)S(1)}, f32[13,8,128]{2,1,0:T(8,128)S(1)}, u32[]{:S(2)}, u32[]{:S(2)}) collective-permute-start(f32[13,8,128]{2,1,0:T(8,128)S(1)} %get-tuple-element.10), channel_id=1, source_target_pairs={{0,4},{4,0},{8,12},{12,8},{16,20},{20,16},{24,28},{28,24},{32,36},... | collective-permute-start | bytes 159752 | tf_op jit(solution)/shard_map/ppermute | solution.py:354
  5.7 0.7 collective-permute-start.1
  6.4 0.8 %collective-permute-done.from_y = f32[13,8,128]{2,1,0:T(8,128)S(1)} collective-permute-done((f32[13,8,128]{2,1,0:T(8,128)S(1)}, f32[13,8,128]{2,1,0:T(8,128)S(1)}, u32[]{:S(2)}, u32[]{:S(2)}) %collective-permute-start) | collective-permute-done | bytes 53280 | tf_op jit(solution)/shard_map/ppermute | solution.py:354
  7.2 0.0 collective-permute-done.1.from_z
  7.2 6.7 %collective-permute-start.3 = (f32[78,8,128]{2,1,0:T(8,128)S(1)}, f32[78,8,128]{2,1,0:T(8,128)S(1)}, u32[]{:S(2)}, u32[]{:S(2)}) collective-permute-start(f32[78,8,128]{2,1,0:T(8,128)S(1)} %widen_kernel.1.full), channel_id=1, source_target_pairs={{1,2},{2,1},{5,6},{6,5},{9,10},{10,9},{13,14},{14,13},{17,18},{18,... | collective-permute-start | bytes 958472 | tf_op jit(solution)/shard_map/ppermute | solution.py:356
  13.9 3.2 %collective-permute-start.2 = (f32[78,8,128]{2,1,0:T(8,128)S(1)}, f32[78,8,128]{2,1,0:T(8,128)S(1)}, u32[]{:S(2)}, u32[]{:S(2)}) collective-permute-start(f32[78,8,128]{2,1,0:T(8,128)S(1)} %widen_kernel.1.full), channel_id=1, source_target_pairs={{0,1},{1,0},{2,3},{3,2},{4,5},{5,4},{6,7},{7,6},{8,9},{9,8},{10,11... | collective-permute-start | bytes 958472 | tf_op jit(solution)/shard_map/ppermute | solution.py:357
  17.2 1.4 %collective-permute-done.3.from_b = f32[78,8,128]{2,1,0:T(8,128)S(1)} collective-permute-done((f32[78,8,128]{2,1,0:T(8,128)S(1)}, f32[78,8,128]{2,1,0:T(8,128)S(1)}, u32[]{:S(2)}, u32[]{:S(2)}) %collective-permute-start.3) | collective-permute-done | bytes 319520 | tf_op jit(solution)/shard_map/ppermute | solution.py:356
  18.6 0.0 collective-permute-done.2.from_a
  18.6 7.3 %stencil_kernel.1 = (f32[24,9216]{1,0:T(8,128)S(1)}, f32[32,8,128]{2,1,0:T(8,128)S(1)}) custom-call(f32[78,8,128]{2,1,0:T(8,128)S(1)} %widen_kernel.1.full, f32[78,8,128]{2,1,0:T(8,128)S(1)} %collective-permute-done.2.from_a, f32[78,8,128]{2,1,0:T(8,128)S(1)} %collective-permute-done.3.from_b), custom_call_target="tpu_custom_call" | custom-call | tf_op jit(solution)/shard_map/stencil_kernel/pallas_call | solution.py:49
  25.9 25.8 %all_to_all.10.parts = f32[32,8,128]{2,1,0:T(8,128)S(1)} all-to-all(f32[32,8,128]{2,1,0:T(8,128)S(1)} %get-tuple-element.12), channel_id=1, replica_groups=mesh['tile_0'=4,'tile_1'=16,'tile_2'=2,'layer_0'=2,'layer_1'=2] {'tile_0..., dimensions={0} | all-to-all | bytes 262144 | tf_op jit(solution)/shard_map/all_to_all | solution.py:371
  51.7 20.6 %all_to_all.11.parts = f32[16,8,128]{2,1,0:T(8,128)S(1)} all-to-all(f32[16,8,128]{2,1,0:T(8,128)S(1)} %total_kernel.1), channel_id=1, replica_groups=mesh['tile_0'=4,'tile_1'=16,'tile_2'=2,'layer_0'=2,'layer_1'=2] {'tile_1'}, dimensions={0} | all-to-all | bytes 131072 | tf_op jit(solution)/shard_map/all_to_all | solution.py:373
  72.3 3.3 %final_kernel.1 = (f32[384,128]{1,0:T(8,128)}, f32[384,128]{1,0:T(8,128)}) custom-call(f32[16,8,128]{2,1,0:T(8,128)S(1)} %all_to_all.11.parts, f32[24,9216]{1,0:T(8,128)S(1)} %get-tuple-element.13.block), custom_call_target="tpu_custom_call" | custom-call | tf_op jit(solution)/shard_map/final_kernel/pallas_call | solution.py:49
  (2 shorter events, 0.1 us)
Async XLA Ops:
  1.7 5.5 %collective-permute-start = (f32[13,8,128]{2,1,0:T(8,128)S(1)}, f32[13,8,128]{2,1,0:T(8,128)S(1)}, u32[]{:S(2)}, u32[]{:S(2)}) collective-permute-start(f32[13,8,128]{2,1,0:T(8,128)S(1)} %get-tuple-element.10), channel_id=1, source_target_pairs={{0,4},{4,0},{8,12},{12,8},{16,20},{20,16},{24,28},{28,24},{32,36},... | collective-permute-start | bytes 159752 | tf_op jit(solution)/shard_map/ppermute | solution.py:354
  5.7 1.5 %collective-permute-start.1 = (f32[13,8,128]{2,1,0:T(8,128)S(1)}, f32[13,8,128]{2,1,0:T(8,128)S(1)}, u32[]{:S(2)}, u32[]{:S(2)}) collective-permute-start(f32[13,8,128]{2,1,0:T(8,128)S(1)} %get-tuple-element.11), channel_id=1, source_target_pairs={{4,8},{8,4},{12,16},{16,12},{20,24},{24,20},{28,32},{32,28},{36,40... | collective-permute-start | bytes 159752 | tf_op jit(solution)/shard_map/ppermute | solution.py:353
  7.2 11.4 %collective-permute-start.3 = (f32[78,8,128]{2,1,0:T(8,128)S(1)}, f32[78,8,128]{2,1,0:T(8,128)S(1)}, u32[]{:S(2)}, u32[]{:S(2)}) collective-permute-start(f32[78,8,128]{2,1,0:T(8,128)S(1)} %widen_kernel.1.full), channel_id=1, source_target_pairs={{1,2},{2,1},{5,6},{6,5},{9,10},{10,9},{13,14},{14,13},{17,18},{18,... | collective-permute-start | bytes 958472 | tf_op jit(solution)/shard_map/ppermute | solution.py:356
  13.9 4.7 %collective-permute-start.2 = (f32[78,8,128]{2,1,0:T(8,128)S(1)}, f32[78,8,128]{2,1,0:T(8,128)S(1)}, u32[]{:S(2)}, u32[]{:S(2)}) collective-permute-start(f32[78,8,128]{2,1,0:T(8,128)S(1)} %widen_kernel.1.full), channel_id=1, source_target_pairs={{0,1},{1,0},{2,3},{3,2},{4,5},{5,4},{6,7},{7,6},{8,9},{9,8},{10,11... | collective-permute-start | bytes 958472 | tf_op jit(solution)/shard_map/ppermute | solution.py:357

commit v3 on v2

v3 whole, which is shorter than its diff:
```python
import jax
import jax.numpy as jnp
from jax import lax
from jax.experimental import pallas as pl
from jax.experimental.pallas import tpu as pltpu
from jax.sharding import Mesh
from jax.sharding import PartitionSpec as P

TILE = ("tile_0", "tile_1", "tile_2")
LAYER = ("layer_0", "layer_1")
PLANE = ("tile_0", "tile_2", "layer_0", "layer_1")
COLUMN = "tile_1"

PROBES = 8
OWN_Z = 2
OWN_X = 8
WIDE_X = OWN_X + 4
SPAN = 128
ROWS = 3 * OWN_Z * OWN_X
EDGE = 13
FULL = 70
SIDE = 6 * WIDE_X
HALF = 3 * OWN_X
F32 = jnp.float32
HIGHEST = lax.Precision.HIGHEST


def vregs(*shape):
    return pltpu.VMEM((*shape, 8, SPAN), F32)


def call(kernel, out_shape, scratch=(), smem=(), outside=()):
    def run(*args):
        specs = [
            pl.BlockSpec(memory_space=pltpu.SMEM if i in smem else pltpu.VMEM)
            for i in range(len(args))
        ]
        args = [
            arg
            if i in smem or i in outside
            else pltpu.with_memory_space_constraint(arg, pltpu.VMEM)
            for i, arg in enumerate(args)
        ]
        outs = out_shape if isinstance(out_shape, (list, tuple)) else None
        out_specs = (
            [pl.BlockSpec(memory_space=pltpu.VMEM)] * len(outs)
            if outs
            else pl.BlockSpec(memory_space=pltpu.VMEM)
        )
        return pl.pallas_call(
            kernel,
            out_shape=out_shape,
            in_specs=specs,
            out_specs=out_specs,
            scratch_shapes=list(scratch),
            name=kernel.__name__,
        )(*args)

    return run


def pack_kernel(lame, probes, material, own, to_y, to_z):
    odd = lax.axis_index("tile_2") == 1
    for z in range(OWN_Z):
        for x in range(OWN_X):
            for c in range(3):
                own[(z * OWN_X + x) * 3 + c] = probes[
                    pl.ds((c * OWN_Z + z) * OWN_X + x, PROBES, stride=ROWS), :
                ]
    fields = {}
    for z in range(OWN_Z):
        kinds = material[z]
        for k in range(2):
            value = jnp.where(
                kinds == 0, lame[k, 0], jnp.where(kinds == 1, lame[k, 1], lame[k, 2])
            )
            fields[k, z] = value * (1.0 / 16.0)
            own[48 + k * 2 + z] = fields[k, z]
    first_y = jnp.where(odd, 0, OWN_X - 2)
    first_z = jnp.where(odd, OWN_X - 2, 0)
    for first, to in ((first_y, to_y), (first_z, to_z)):
        for z in range(OWN_Z):
            for xx in range(2):
                for c in range(3):
                    to[(z * 2 + xx) * 3 + c] = own[(z * OWN_X + first + xx) * 3 + c]
    low = jnp.concatenate([fields[k, z][0:2] for k in range(2) for z in range(2)], 0)
    high = jnp.concatenate([fields[k, z][6:8] for k in range(2) for z in range(2)], 0)
    to_y[12] = jnp.where(odd, low, high)
    to_z[12] = jnp.where(odd, high, low)


def stress(modes, lam, mu):
    a, b, e, p, q, r, t = modes
    third = 1.0 / 3.0
    lam3 = lam * third
    mu3 = mu * third
    both = mu + lam3
    top = (4.0 * mu + lam) * (1.0 / 9.0)
    twice = mu + mu
    trace = lam * (a[0] + b[1] + e[2])
    s01 = mu * (b[0] + a[1])
    s02 = mu * (e[0] + a[2])
    s12 = mu * (e[1] + b[2])
    aa = (twice * a[0] + trace, s01, s02)
    bb = (s01, twice * b[1] + trace, s12)
    ee = (s02, s12, twice * e[2] + trace)
    mixed = p[2] + q[1] + r[0]
    pp = (both * p[0] + lam3 * r[2], both * p[1] + lam3 * q[2], mu3 * (p[2] + mixed))
    qq = (both * q[0] + lam3 * r[1], mu3 * (q[1] + mixed), both * q[2] + lam3 * p[1])
    rr = (mu3 * (r[0] + mixed), both * r[1] + lam3 * q[0], both * r[2] + lam3 * p[0])
    tt = tuple(top * t[c] for c in range(3))
    return aa, bb, ee, pp, qq, rr, tt


def along_x(values):
    s0, d0, s1, d1 = values
    return (s0 + s1, s1 - s0, d0 + d1, d1 - d0)


def element(lower, upper, lam, mu):
    modes = tuple(
        tuple(
            upper[c][kind] - lower[c][kind] if minus else upper[c][kind] + lower[c][kind]
            for c in range(3)
        )
        for kind, minus in (
            (0, True),
            (1, False),
            (2, False),
            (1, True),
            (2, True),
            (3, False),
            (3, True),
        )
    )
    return stress(modes, lam, mu)


def to_lower(duals, c):
    aa, bb, ee, pp, qq, rr, tt = duals
    return (-aa[c], bb[c] - pp[c], ee[c] - qq[c], rr[c] - tt[c])


def to_upper(duals, c):
    aa, bb, ee, pp, qq, rr, tt = duals
    return (aa[c], bb[c] + pp[c], ee[c] + qq[c], rr[c] + tt[c])


def edge_masks():
    lanes = lax.broadcasted_iota(jnp.int32, (8, SPAN), 1)
    not_last = jnp.where(lanes == SPAN - 1, 0.0, 1.0).astype(F32)
    not_first = jnp.where(lanes == 0, 0.0, 1.0).astype(F32)
    return not_last, not_first

def spread(value, not_last):
    after = pltpu.roll(value, SPAN - 1, 1) * not_last
    return value + after, after - value


class Column:
    def __init__(self, not_first):
        self.not_first = not_first
        self.left = {}

    def node(self, key, parts):
        ss, ds, sd, dd = parts
        now_s, now_d = ss - ds, sd - dd
        if key in self.left:
            now_s = now_s + self.left[key][0]
            now_d = now_d + self.left[key][1]
        self.left[key] = (ss + ds, sd + dd)
        return (now_s - now_d) + pltpu.roll(now_s + now_d, 1, 1) * self.not_first


def nodes_of(ref, x, c, sign=None):
    at = (x * 3 + c) * 2
    values = (ref[at], ref[at + 1], ref[at + 6], ref[at + 7])
    if sign is not None and c == 0:
        values = tuple(sign * value for value in values)
    return along_x(values)


def layer_of(ref, x, sign=None):
    return [nodes_of(ref, x, c, sign) for c in range(3)]


def moduli(rows, x):
    return tuple(jnp.broadcast_to(rows[at : at + 1, :], (8, SPAN)) for at in (x, 16 + x))


def inner_kernel(
    own, from_y, from_z, pairs_a, pairs_b, base_a, base_b, rows, to_a, to_b, probes_block
):
    odd = lax.axis_index("tile_2") == 1
    first_core = lax.axis_index("layer_1") == 0
    sign = jnp.where(first_core, -1.0, 1.0).astype(F32)
    not_last, not_first = edge_masks()
    for x in range(WIDE_X):
        for c in range(3):
            values = []
            for z in range(OWN_Z):
                if x < 2:
                    at = (z * 2 + x) * 3 + c
                    values.append(jnp.where(odd, from_y[at], from_z[at]))
                elif x < 10:
                    values.append(own[(z * OWN_X + x - 2) * 3 + c])
                else:
                    at = (z * 2 + x - 10) * 3 + c
                    values.append(jnp.where(odd, from_z[at], from_y[at]))
            near_a = jnp.where(first_core, values[1], values[0])
            near_b = jnp.where(first_core, values[0], values[1])
            to_a[x * 3 + c] = near_a
            to_b[x * 3 + c] = near_b
            for half, pairs, value in ((0, pairs_a, near_a), (1, pairs_b, near_b)):
                pairs[(x * 3 + c) * 2], pairs[(x * 3 + c) * 2 + 1] = spread(value, not_last)
                if 2 <= x < 10:
                    at = (half * HALF + (x - 2) * 3 + c) * SPAN
                    probes_block[:, at : at + SPAN] = value
    left = jnp.where(odd, from_y[12], from_z[12])
    right = jnp.where(odd, from_z[12], from_y[12])
    for z in range(OWN_Z):
        for k in range(2):
            at = (z * 2 + k) * 16
            rows[at + 2 : at + 10, :] = own[48 + k * 2 + z]
            rows[at : at + 2, :] = left[k * 4 + z * 2 : k * 4 + z * 2 + 2]
            rows[at + 10 : at + 12, :] = right[k * 4 + z * 2 : k * 4 + z * 2 + 2]
            rows[at + 12 : at + 16, :] = jnp.zeros((4, SPAN), F32)
    for i in range(4):
        first, second = rows[i * 8 : i * 8 + 8, :], rows[32 + i * 8 : 40 + i * 8, :]
        to_a[66 + i] = jnp.where(first_core, second, first)
        to_b[66 + i] = jnp.where(first_core, first, second)
    column = Column(not_first)
    for x in range(WIDE_X - 1):
        duals = element(layer_of(pairs_a, x, sign), layer_of(pairs_b, x, sign), *moduli(rows, x))
        for c in range(3):
            force_a = column.node((0, c), to_lower(duals, c))
            force_b = column.node((1, c), to_upper(duals, c))
            if x:
                if c == 0:
                    force_a, force_b = sign * force_a, sign * force_b
                base_a[x * 3 + c] = force_a
                base_b[x * 3 + c] = force_b
                to_a[33 + x * 3 + c] = force_a
                to_b[33 + x * 3 + c] = force_b


def side_pass(above, other, pairs, base, rows, pairs_other, rows_side, near_one, far_one, one_block, first):
    tile = (lax.axis_index("tile_0") * 16 + lax.axis_index("tile_1")) * 2 + lax.axis_index("tile_2")
    layer = lax.axis_index("layer_0") * 2 + lax.axis_index("layer_1")
    not_last, not_first = edge_masks()
    sign = jnp.where(above, 1.0, -1.0).astype(F32)
    keep_x = jnp.where(tile == 127, 0.0, 1.0).astype(F32)
    keep_z = jnp.where((layer == 3) & above, 0.0, 1.0).astype(F32)
    for x in range(WIDE_X):
        for c in range(3):
            at = (x * 3 + c) * 2
            pairs_other[at], pairs_other[at + 1] = spread(other[x * 3 + c], not_last)
    for i in range(4):
        rows_side[i * 8 : i * 8 + 8, :] = jnp.where(
            above, rows[32 + i * 8 : 40 + i * 8, :], other[66 + i]
        )
    column = Column(not_first)
    for x in range(WIDE_X - 1):
        duals = element(
            layer_of(pairs, x, sign), layer_of(pairs_other, x, sign), *moduli(rows_side, x)
        )
        for c in range(3):
            near = column.node((0, c), to_lower(duals, c))
            far = column.node((1, c), to_upper(duals, c))
            if x:
                if c == 0:
                    near, far = sign * near, sign * far
                near = near + base[x * 3 + c]
                far = (far + other[33 + x * 3 + c]) * keep_z
                if x == 10:
                    near, far = near * keep_x, far * keep_x
                if 2 <= x < 10:
                    at = (first + (x - 2) * 3 + c) * SPAN
                    one_block[:, at : at + SPAN] = near
                at = (x * 3 + c) * 2
                near_one[at], near_one[at + 1] = spread(near, not_last)
                far_one[at], far_one[at + 1] = spread(far, not_last)
    return sign


def side_a_kernel(
    other, pairs, base, rows, near_one, one_block, two_side, pairs_other, rows_side, far_one
):
    above = lax.axis_index("layer_1") == 0
    sign = side_pass(
        above, other, pairs, base, rows, pairs_other, rows_side, near_one, far_one, one_block, 0
    )
    column = Column(edge_masks()[1])
    for x in range(1, WIDE_X - 2):
        duals = element(
            layer_of(near_one, x, sign), layer_of(far_one, x, sign), *moduli(rows_side, x)
        )
        for c in range(3):
            force = column.node(c, to_lower(duals, c))
            if x > 1:
                two_side[(x - 2) * 3 + c] = sign * force if c == 0 else force


def side_b_kernel(
    other,
    pairs,
    base,
    rows,
    near_a,
    one_block_a,
    two_a,
    probes_block,
    block,
    message,
    pairs_other,
    rows_side,
    near_one,
    far_one,
    one_block,
):
    above = lax.axis_index("layer_1") == 1
    block[0:8, :] = probes_block[...]
    block[8:16, 0 : HALF * SPAN] = one_block_a[...]
    sign = side_pass(
        above, other, pairs, base, rows, pairs_other, rows_side, near_one, far_one, one_block, 0
    )
    block[8:16, HALF * SPAN :] = one_block[...]
    column = Column(edge_masks()[1])
    for x in range(1, WIDE_X - 2):
        outer = element(
            layer_of(near_one, x, sign), layer_of(far_one, x, sign), *moduli(rows_side, x)
        )
        inner = element(layer_of(near_a, x, sign), layer_of(near_one, x, sign), *moduli(rows, x))
        for c in range(3):
            both = zip(to_lower(outer, c), to_upper(inner, c))
            force_b = column.node((1, c), tuple(one + two for one, two in both))
            force_a = column.node((0, c), to_lower(inner, c))
            if x > 1:
                if c == 0:
                    force_a, force_b = sign * force_a, sign * force_b
                at = ((x - 2) * 3 + c) * SPAN
                block[16:24, at : at + SPAN] = force_a + two_a[(x - 2) * 3 + c]
                at = at + HALF * SPAN
                block[16:24, at : at + SPAN] = force_b
    every = block[...]
    grams = lax.dot_general(
        every[0:16], every, (((1,), (1,)), ((), ())), precision=HIGHEST, preferred_element_type=F32
    )
    lanes = lax.broadcasted_iota(jnp.int32, (8, SPAN), 1)
    wide = jnp.concatenate([grams, jnp.zeros((16, SPAN - 24), F32)], 1)
    packed = jnp.where(lanes < 16, wide[0:8], pltpu.roll(wide[8:16], 8, 1))
    for i in range(message.shape[0]):
        message[i] = packed


def total_kernel(parts, message):
    total = parts[0]
    for i in range(1, parts.shape[0]):
        total = total + parts[i]
    for i in range(message.shape[0]):
        message[i] = total


def eliminate(table, first):
    rows = lax.broadcasted_iota(jnp.int32, (8, SPAN), 0)
    for k in range(8):
        pivot_row = jnp.broadcast_to(table[k : k + 1, :], (8, SPAN))
        column = jnp.broadcast_to(table[:, first + k : first + k + 1], (8, SPAN))
        pivot = jnp.broadcast_to(table[k : k + 1, first + k : first + k + 1], (8, SPAN))
        scaled = pivot_row / pivot
        table = jnp.where(rows == k, scaled, table - column * scaled)
    return table


def times(left, first, right):
    total = None
    for k in range(8):
        column = jnp.broadcast_to(left[:, first + k : first + k + 1], (8, SPAN))
        row = jnp.broadcast_to(right[k : k + 1, :], (8, SPAN))
        total = column * row if total is None else total + column * row
    return total


def final_kernel(parts, block, solution_rows, residual_rows):
    table = parts[0]
    for i in range(1, parts.shape[0]):
        table = table + parts[i]
    lanes = lax.broadcasted_iota(jnp.int32, (8, SPAN), 1)
    solved = eliminate(table, 8)
    product = times(table, 16, solved)
    shifted = pltpu.roll(table, SPAN - 8, 1)
    second = jnp.where(lanes < 8, product - shifted, shifted - product)
    coef_c = jnp.where(lanes < 8, eliminate(second, 16), 0.0)
    coef_b = jnp.where(lanes < 8, solved + times(solved, 16, coef_c), 0.0)
    coefs = jnp.concatenate(
        [coef_b, -coef_c - pltpu.roll(coef_b, 8, 1), pltpu.roll(coef_c, 8, 1)], 0
    )[:, 0:16]
    every = block[...]
    mixed = lax.dot_general(
        coefs, every, (((0,), (0,)), ((), ())), precision=HIGHEST, preferred_element_type=F32
    )
    first_core = lax.axis_index("layer_1") == 0
    for half in range(2):
        layer = jnp.where(first_core, 1 - half, half)
        for x in range(OWN_X):
            for c in range(3):
                at = (half * HALF + x * 3 + c) * SPAN
                rows = pl.ds((c * OWN_Z + layer) * OWN_X + x, PROBES, stride=ROWS)
                solution_rows[rows, :] = mixed[0:8, at : at + SPAN]
                residual_rows[rows, :] = every[0:8, at : at + SPAN] + mixed[8:16, at : at + SPAN]


def body(probes, material, lame_pairs):
    tiles = lax.axis_size(TILE)
    in_y = [(i, i ^ 1) for i in range(tiles)]
    in_z = [(i, ((i + 1) ^ 1) - 1) for i in range(1, tiles - 1)]
    in_core = [(0, 1), (1, 0), (2, 3), (3, 2)]
    in_chip = [(1, 2), (2, 1)]
    own, to_y, to_z = call(pack_kernel, (vregs(52), vregs(EDGE), vregs(EDGE)), smem=(0,), outside=(1, 2))(
        lame_pairs.T, probes.reshape(PROBES * ROWS, SPAN), material
    )
    from_z = lax.ppermute(to_z, TILE, in_z)
    from_y = lax.ppermute(to_y, TILE, in_y)
    moduli_rows = pltpu.VMEM((64, SPAN), F32)
    half_block = pltpu.VMEM((8, HALF * SPAN), F32)
    pairs_a, pairs_b, base_a, base_b, rows, to_a, to_b, probes_block = call(
        inner_kernel,
        (
            vregs(SIDE),
            vregs(SIDE),
            vregs(36),
            vregs(36),
            moduli_rows,
            vregs(FULL),
            vregs(FULL),
            pltpu.VMEM((8, 2 * HALF * SPAN), F32),
        ),
    )(own, from_y, from_z)
    from_b = lax.ppermute(to_b, LAYER, in_chip)
    from_a = lax.ppermute(to_a, LAYER, in_core)
    planes = lax.axis_size(PLANE)
    columns = lax.axis_size(COLUMN)
    scratch = (pltpu.VMEM((SIDE, 8, SPAN), F32), pltpu.VMEM((32, SPAN), F32))
    near_a, one_block_a, two_a = call(
        side_a_kernel,
        (vregs(SIDE), half_block, vregs(HALF)),
        scratch=(*scratch, pltpu.VMEM((SIDE, 8, SPAN), F32)),
    )(from_a, pairs_a, base_a, rows)
    block, message = call(
        side_b_kernel,
        (pltpu.VMEM((24, 2 * HALF * SPAN), F32), vregs(planes)),
        scratch=(
            *scratch,
            pltpu.VMEM((SIDE, 8, SPAN), F32),
            pltpu.VMEM((SIDE, 8, SPAN), F32),
            half_block,
        ),
    )(from_b, pairs_b, base_b, rows, near_a, one_block_a, two_a, probes_block)
    parts = lax.all_to_all(message, PLANE, 0, 0, tiled=True)
    message = call(total_kernel, vregs(columns))(parts)
    parts = lax.all_to_all(message, COLUMN, 0, 0, tiled=True)
    rows = jax.ShapeDtypeStruct((PROBES * ROWS, SPAN), F32)
    solution_rows, residual_rows = call(final_kernel, (rows, rows))(parts, block)
    return solution_rows.reshape(probes.shape), residual_rows.reshape(probes.shape)


def solution(mesh):
    split = Mesh(
        mesh.devices.reshape(4, 16, 2, 2, 2), ("tile_0", "tile_1", "tile_2", "layer_0", "layer_1")
    )
    spread = P(None, None, LAYER, TILE, None)
    return jax.shard_map(
        body,
        mesh=split,
        in_specs=(spread, P(LAYER, TILE, None), P()),
        out_specs=(spread, spread),
        check_vma=False,
    )
```

time: 75.9 us -> 72.1 us (0.950)
  blocking collectives: 46.4 us -> 40.6 us
  waiting for transfers between devices: 2.26 us -> 7.64 us
  Pallas kernels: 11.7 us -> 7.05 us
  starting transfers between devices: 14.6 us -> 15.8 us
    all_to_all x1, blocking collectives: 25.8 us -> 19.9 us  [body(): parts = lax.all_to_all(message, PLANE, 0, 0, tiled=True)]
    ppermute x2, waiting for transfers between devices: 1.42 us -> 6.8 us  [the longest x1 6.8 us: body(): from_b = lax.ppermute(to_b, LAYER, in_chip)]
    pallas_call x5 -> x6, Pallas kernels: 11.7 us -> 7.05 us  [run(): pl.pallas_call(kernel, out_shape=out_shape, in_specs=specs, out_specs=out...]
    ppermute x2, starting transfers between devices: 9.92 us -> 11.2 us  [the longest x1 9.23 us: body(): from_a = lax.ppermute(to_a, LAYER, in_core)]
  transfers between devices with their start and end apart: 4 -> 4, of which waited for: 2 -> 2; matrix products, arithmetic and copies ran while one was open for 0% -> 0% of each run, Pallas kernels for 0% -> 1%
where the time goes in v3:
time: 72.1 us; the launch traced here: 71.9 us
  blocking collectives  40.6 us (56%)
  starting transfers between devices  15.8 us (22%)
  waiting for transfers between devices  7.64 us (11%)
  Pallas kernels  7.05 us (10%)
    all_to_all x1, blocking collectives, body(): parts = lax.all_to_all(message, COLUMN, 0, 0, tiled=True)  20.7 us
    all_to_all x1, blocking collectives, body(): parts = lax.all_to_all(message, PLANE, 0, 0, tiled=True)  19.9 us
    ppermute x1, starting transfers between devices, body(): from_a = lax.ppermute(to_a, LAYER, in_core)  9.23 us
    pallas_call x6, Pallas kernels, run(): pl.pallas_call(kernel, out_shape=out_shape, in_specs=specs, out_specs=out...  7.05 us
    ppermute x1, waiting for transfers between devices, body(): from_b = lax.ppermute(to_b, LAYER, in_chip)  6.8 us
    ppermute x1, starting transfers between devices, body(): from_y = lax.ppermute(to_y, TILE, in_y)  4.02 us
    ppermute x1, starting transfers between devices, body(): from_b = lax.ppermute(to_b, LAYER, in_chip)  1.92 us
  transfers between devices with their start and end apart: 4, of which 2 were waited for; matrix products, arithmetic and copies ran while one was open for 0% of the time, Pallas kernels for 1%

profile of v3, /device:TPU:1, one launch (start us, length us, event | category | flops | bytes accessed | tf_op | source)
XLA Modules:
  0.0 71.9 jit_solution(1838211276353647367)
XLA Ops:
  0.6 1.0 %pack_kernel.1 = (f32[52,8,128]{2,1,0:T(8,128)S(1)}, f32[13,8,128]{2,1,0:T(8,128)S(1)}, f32[13,8,128]{2,1,0:T(8,128)S(1)}) custom-call(f32[2,3]{1,0:T(2,128)} %bitcast.5, f32[384,128]{1,0:T(8,128)} %bitcast.4, s32[2,8,128]{2,1,0:T(8,128)} %material.1), custom_call_target="tpu_custom_call" | custom-call | tf_op jit(solution)/shard_map/pack_kernel/pallas_call | solution.py:50
  1.7 4.0 %collective-permute-start = (f32[13,8,128]{2,1,0:T(8,128)S(1)}, f32[13,8,128]{2,1,0:T(8,128)S(1)}, u32[]{:S(2)}, u32[]{:S(2)}) collective-permute-start(f32[13,8,128]{2,1,0:T(8,128)S(1)} %get-tuple-element.21), channel_id=1, source_target_pairs={{0,4},{4,0},{8,12},{12,8},{16,20},{20,16},{24,28},{28,24},{32,36},... | collective-permute-start | bytes 159752 | tf_op jit(solution)/shard_map/ppermute | solution.py:423
  5.7 0.7 collective-permute-start.1
  6.4 0.8 %collective-permute-done.from_y = f32[13,8,128]{2,1,0:T(8,128)S(1)} collective-permute-done((f32[13,8,128]{2,1,0:T(8,128)S(1)}, f32[13,8,128]{2,1,0:T(8,128)S(1)}, u32[]{:S(2)}, u32[]{:S(2)}) %collective-permute-start) | collective-permute-done | bytes 53280 | tf_op jit(solution)/shard_map/ppermute | solution.py:423
  7.2 0.0 collective-permute-done.1.from_z
  7.2 0.5 inner_kernel.1
  7.7 9.2 %collective-permute-start.3 = (f32[70,8,128]{2,1,0:T(8,128)S(1)}, f32[70,8,128]{2,1,0:T(8,128)S(1)}, u32[]{:S(2)}, u32[]{:S(2)}) collective-permute-start(f32[70,8,128]{2,1,0:T(8,128)S(1)} %get-tuple-element.27), channel_id=1, source_target_pairs={{0,1},{1,0},{2,3},{3,2},{4,5},{5,4},{6,7},{7,6},{8,9},{9,8},{10,11... | collective-permute-start | bytes 860168 | tf_op jit(solution)/shard_map/ppermute | solution.py:440
  16.9 1.9 %collective-permute-start.2 = (f32[70,8,128]{2,1,0:T(8,128)S(1)}, f32[70,8,128]{2,1,0:T(8,128)S(1)}, u32[]{:S(2)}, u32[]{:S(2)}) collective-permute-start(f32[70,8,128]{2,1,0:T(8,128)S(1)} %get-tuple-element.23), channel_id=1, source_target_pairs={{1,2},{2,1},{5,6},{6,5},{9,10},{10,9},{13,14},{14,13},{17,18},{18,... | collective-permute-start | bytes 860168 | tf_op jit(solution)/shard_map/ppermute | solution.py:439
  18.8 0.0 collective-permute-done.3.other
  18.9 0.7 side_a_kernel.1
  19.6 6.8 %collective-permute-done.2.other = f32[70,8,128]{2,1,0:T(8,128)S(1)} collective-permute-done((f32[70,8,128]{2,1,0:T(8,128)S(1)}, f32[70,8,128]{2,1,0:T(8,128)S(1)}, u32[]{:S(2)}, u32[]{:S(2)}) %collective-permute-start.2) | collective-permute-done | bytes 286752 | tf_op jit(solution)/shard_map/ppermute | solution.py:439
  26.4 1.5 %side_b_kernel.1 = (f32[24,6144]{1,0:T(8,128)S(1)}, f32[32,8,128]{2,1,0:T(8,128)S(1)}) custom-call(f32[70,8,128]{2,1,0:T(8,128)S(1)} %collective-permute-done.2.other, f32[72,8,128]{2,1,0:T(8,128)S(1)} %get-tuple-element.24.pairs, f32[36,8,128]{2,1,0:T(8,128)S(1)} %get-tuple-element.25.base, f32[64,128]{1,0:T(8,128)S(1)} %get-tuple-element.26.rows, ...), custom_call_target="tpu_custom_call" | custom-call | tf_op jit(solution)/shard_map/side_b_kernel/pallas_call | solution.py:50
  27.9 19.9 %all_to_all.10.parts = f32[32,8,128]{2,1,0:T(8,128)S(1)} all-to-all(f32[32,8,128]{2,1,0:T(8,128)S(1)} %get-tuple-element.34), channel_id=1, replica_groups=mesh['tile_0'=4,'tile_1'=16,'tile_2'=2,'layer_0'=2,'layer_1'=2] {'tile_0..., dimensions={0} | all-to-all | bytes 262144 | tf_op jit(solution)/shard_map/all_to_all | solution.py:459
  47.8 20.7 %all_to_all.11.parts = f32[16,8,128]{2,1,0:T(8,128)S(1)} all-to-all(f32[16,8,128]{2,1,0:T(8,128)S(1)} %total_kernel.1), channel_id=1, replica_groups=mesh['tile_0'=4,'tile_1'=16,'tile_2'=2,'layer_0'=2,'layer_1'=2] {'tile_1'}, dimensions={0} | all-to-all | bytes 131072 | tf_op jit(solution)/shard_map/all_to_all | solution.py:461
  68.6 3.3 %final_kernel.1 = (f32[384,128]{1,0:T(8,128)}, f32[384,128]{1,0:T(8,128)}) custom-call(f32[16,8,128]{2,1,0:T(8,128)S(1)} %all_to_all.11.parts, f32[24,6144]{1,0:T(8,128)S(1)} %get-tuple-element.35.block), custom_call_target="tpu_custom_call" | custom-call | tf_op jit(solution)/shard_map/final_kernel/pallas_call | solution.py:50
  (1 shorter events, 0.0 us)
Async XLA Ops:
  1.7 5.5 %collective-permute-start = (f32[13,8,128]{2,1,0:T(8,128)S(1)}, f32[13,8,128]{2,1,0:T(8,128)S(1)}, u32[]{:S(2)}, u32[]{:S(2)}) collective-permute-start(f32[13,8,128]{2,1,0:T(8,128)S(1)} %get-tuple-element.21), channel_id=1, source_target_pairs={{0,4},{4,0},{8,12},{12,8},{16,20},{20,16},{24,28},{28,24},{32,36},... | collective-permute-start | bytes 159752 | tf_op jit(solution)/shard_map/ppermute | solution.py:423
  5.7 1.5 %collective-permute-start.1 = (f32[13,8,128]{2,1,0:T(8,128)S(1)}, f32[13,8,128]{2,1,0:T(8,128)S(1)}, u32[]{:S(2)}, u32[]{:S(2)}) collective-permute-start(f32[13,8,128]{2,1,0:T(8,128)S(1)} %get-tuple-element.22), channel_id=1, source_target_pairs={{4,8},{8,4},{12,16},{16,12},{20,24},{24,20},{28,32},{32,28},{36,40... | collective-permute-start | bytes 159752 | tf_op jit(solution)/shard_map/ppermute | solution.py:422
  7.7 11.2 %collective-permute-start.3 = (f32[70,8,128]{2,1,0:T(8,128)S(1)}, f32[70,8,128]{2,1,0:T(8,128)S(1)}, u32[]{:S(2)}, u32[]{:S(2)}) collective-permute-start(f32[70,8,128]{2,1,0:T(8,128)S(1)} %get-tuple-element.27), channel_id=1, source_target_pairs={{0,1},{1,0},{2,3},{3,2},{4,5},{5,4},{6,7},{7,6},{8,9},{9,8},{10,11... | collective-permute-start | bytes 860168 | tf_op jit(solution)/shard_map/ppermute | solution.py:440
  16.9 9.5 %collective-permute-start.2 = (f32[70,8,128]{2,1,0:T(8,128)S(1)}, f32[70,8,128]{2,1,0:T(8,128)S(1)}, u32[]{:S(2)}, u32[]{:S(2)}) collective-permute-start(f32[70,8,128]{2,1,0:T(8,128)S(1)} %get-tuple-element.23), channel_id=1, source_target_pairs={{1,2},{2,1},{5,6},{6,5},{9,10},{10,9},{13,14},{14,13},{17,18},{18,... | collective-permute-start | bytes 860168 | tf_op jit(solution)/shard_map/ppermute | solution.py:439

commit v4 on v3

--- a/solution.py
+++ b/solution.py
@@ -5,6 +5,7 @@
 from jax.experimental.pallas import tpu as pltpu
 from jax.sharding import Mesh
 from jax.sharding import PartitionSpec as P
+
 
 TILE = ("tile_0", "tile_1", "tile_2")
 LAYER = ("layer_0", "layer_1")
@@ -53,7 +54,6 @@
             in_specs=specs,
             out_specs=out_specs,
             scratch_shapes=list(scratch),
-            name=kernel.__name__,
         )(*args)
 
     return run
@@ -151,6 +151,7 @@
     not_last = jnp.where(lanes == SPAN - 1, 0.0, 1.0).astype(F32)
     not_first = jnp.where(lanes == 0, 0.0, 1.0).astype(F32)
     return not_last, not_first
+
 
 def spread(value, not_last):
     after = pltpu.roll(value, SPAN - 1, 1) * not_last
@@ -349,8 +350,19 @@
     lanes = lax.broadcasted_iota(jnp.int32, (8, SPAN), 1)
     wide = jnp.concatenate([grams, jnp.zeros((16, SPAN - 24), F32)], 1)
     packed = jnp.where(lanes < 16, wide[0:8], pltpu.roll(wide[8:16], 8, 1))
+    packed = turned(jnp.where(lanes < 32, packed, 0.0), 1)
+    halves = [packed[i : i + 1] + packed[i + 1 : i + 2] for i in (0, 2, 4, 6)]
+    packed = jnp.concatenate([halves[0] + halves[1], halves[2] + halves[3]], 0)
     for i in range(message.shape[0]):
         message[i] = packed
+
+
+def turned(table, way):
+    quarter = lax.broadcasted_iota(jnp.int32, (8, SPAN), 0) & 3
+    result = table
+    for i in range(1, 4):
+        result = jnp.where(quarter == i, pltpu.roll(table, (way * 32 * i) % SPAN, 1), result)
+    return result
 
 
 def total_kernel(parts, message):
@@ -363,12 +375,20 @@
 
 def eliminate(table, first):
     rows = lax.broadcasted_iota(jnp.int32, (8, SPAN), 0)
-    for k in range(8):
-        pivot_row = jnp.broadcast_to(table[k : k + 1, :], (8, SPAN))
-        column = jnp.broadcast_to(table[:, first + k : first + k + 1], (8, SPAN))
-        pivot = jnp.broadcast_to(table[k : k + 1, first + k : first + k + 1], (8, SPAN))
-        scaled = pivot_row / pivot
-        table = jnp.where(rows == k, scaled, table - column * scaled)
+    for k in range(0, 8, 2):
+        top = jnp.broadcast_to(table[k : k + 1, :], (8, SPAN))
+        low = jnp.broadcast_to(table[k + 1 : k + 2, :], (8, SPAN))
+        left = jnp.broadcast_to(table[:, first + k : first + k + 1], (8, SPAN))
+        right = jnp.broadcast_to(table[:, first + k + 1 : first + k + 2], (8, SPAN))
+        p00 = jnp.broadcast_to(left[k : k + 1, :], (8, SPAN))
+        p10 = jnp.broadcast_to(left[k + 1 : k + 2, :], (8, SPAN))
+        p01 = jnp.broadcast_to(right[k : k + 1, :], (8, SPAN))
+        p11 = jnp.broadcast_to(right[k + 1 : k + 2, :], (8, SPAN))
+        scale = 1.0 / (p00 * p11 - p01 * p10)
+        new_top = (p11 * top - p01 * low) * scale
+        new_low = (p00 * low - p10 * top) * scale
+        rest = table - left * new_top - right * new_low
+        table = jnp.where(rows == k, new_top, jnp.where(rows == k + 1, new_low, rest))
     return table
 
 
@@ -382,10 +402,12 @@
 
 
 def final_kernel(parts, block, solution_rows, residual_rows):
-    table = parts[0]
+    total = parts[0]
     for i in range(1, parts.shape[0]):
-        table = table + parts[i]
+        total = total + parts[i]
     lanes = lax.broadcasted_iota(jnp.int32, (8, SPAN), 1)
+    table = jnp.concatenate([jnp.broadcast_to(total[i : i + 1], (4, SPAN)) for i in (0, 1)], 0)
+    table = jnp.where(lanes < 32, turned(table, -1), 0.0)
     solved = eliminate(table, 8)
     product = times(table, 16, solved)
     shifted = pltpu.roll(table, SPAN - 8, 1)
@@ -448,7 +470,7 @@
     )(from_a, pairs_a, base_a, rows)
     block, message = call(
         side_b_kernel,
-        (pltpu.VMEM((24, 2 * HALF * SPAN), F32), vregs(planes)),
+        (pltpu.VMEM((24, 2 * HALF * SPAN), F32), pltpu.VMEM((planes, 2, SPAN), F32)),
         scratch=(
             *scratch,
             pltpu.VMEM((SIDE, 8, SPAN), F32),
@@ -457,7 +479,7 @@
         ),
     )(from_b, pairs_b, base_b, rows, near_a, one_block_a, two_a, probes_block)
     parts = lax.all_to_all(message, PLANE, 0, 0, tiled=True)
-    message = call(total_kernel, vregs(columns))(parts)
+    message = call(total_kernel, pltpu.VMEM((columns, 2, SPAN), F32))(parts)
     parts = lax.all_to_all(message, COLUMN, 0, 0, tiled=True)
     rows = jax.ShapeDtypeStruct((PROBES * ROWS, SPAN), F32)
     solution_rows, residual_rows = call(final_kernel, (rows, rows))(parts, block)

time: 72.1 us -> 71 us (0.985)
  no operation moved by 1% of the time
where the time goes in v4:
time: 71 us; the launch traced here: 70.7 us
  blocking collectives  40.2 us (57%)
  starting transfers between devices  15.8 us (22%)
  waiting for transfers between devices  7.64 us (11%)
  Pallas kernels  6.38 us (9%)
    all_to_all x1, blocking collectives, body(): parts = lax.all_to_all(message, COLUMN, 0, 0, tiled=True)  20.6 us
    all_to_all x1, blocking collectives, body(): parts = lax.all_to_all(message, PLANE, 0, 0, tiled=True)  19.6 us
    ppermute x1, starting transfers between devices, body(): from_a = lax.ppermute(to_a, LAYER, in_core)  9.23 us
    ppermute x1, waiting for transfers between devices, body(): from_b = lax.ppermute(to_b, LAYER, in_chip)  6.8 us
    pallas_call x6, Pallas kernels, run(): pl.pallas_call(kernel, out_shape=out_shape, in_specs=specs, out_specs=out...  6.38 us
    ppermute x1, starting transfers between devices, body(): from_y = lax.ppermute(to_y, TILE, in_y)  4.02 us
    ppermute x1, starting transfers between devices, body(): from_b = lax.ppermute(to_b, LAYER, in_chip)  1.92 us
  transfers between devices with their start and end apart: 4, of which 2 were waited for; matrix products, arithmetic and copies ran while one was open for 0% of the time, Pallas kernels for 1%

profile of v4, /device:TPU:1, one launch (start us, length us, event | category | flops | bytes accessed | tf_op | source)
XLA Modules:
  0.0 70.7 jit_solution(11196932772048330539)
XLA Ops:
  0.6 1.0 %shard_map.50 = (f32[52,8,128]{2,1,0:T(8,128)S(1)}, f32[13,8,128]{2,1,0:T(8,128)S(1)}, f32[13,8,128]{2,1,0:T(8,128)S(1)}) custom-call(f32[2,3]{1,0:T(2,128)} %bitcast.5, f32[384,128]{1,0:T(8,128)} %bitcast.4, s32[2,8,128]{2,1,0:T(8,128)} %material.1), custom_call_target="tpu_custom_call" | custom-call | tf_op jit(solution)/shard_map/pallas_call | solution.py:51
  1.7 4.0 %collective-permute-start = (f32[13,8,128]{2,1,0:T(8,128)S(1)}, f32[13,8,128]{2,1,0:T(8,128)S(1)}, u32[]{:S(2)}, u32[]{:S(2)}) collective-permute-start(f32[13,8,128]{2,1,0:T(8,128)S(1)} %get-tuple-element.21), channel_id=1, source_target_pairs={{0,4},{4,0},{8,12},{12,8},{16,20},{20,16},{24,28},{28,24},{32,36},... | collective-permute-start | bytes 159752 | tf_op jit(solution)/shard_map/ppermute | solution.py:445
  5.7 0.7 collective-permute-start.1
  6.4 0.8 %collective-permute-done.from_y = f32[13,8,128]{2,1,0:T(8,128)S(1)} collective-permute-done((f32[13,8,128]{2,1,0:T(8,128)S(1)}, f32[13,8,128]{2,1,0:T(8,128)S(1)}, u32[]{:S(2)}, u32[]{:S(2)}) %collective-permute-start) | collective-permute-done | bytes 53280 | tf_op jit(solution)/shard_map/ppermute | solution.py:445
  7.2 0.0 collective-permute-done.1.from_z
  7.2 0.5 shard_map.51
  7.7 9.2 %collective-permute-start.3 = (f32[70,8,128]{2,1,0:T(8,128)S(1)}, f32[70,8,128]{2,1,0:T(8,128)S(1)}, u32[]{:S(2)}, u32[]{:S(2)}) collective-permute-start(f32[70,8,128]{2,1,0:T(8,128)S(1)} %get-tuple-element.27), channel_id=1, source_target_pairs={{0,1},{1,0},{2,3},{3,2},{4,5},{5,4},{6,7},{7,6},{8,9},{9,8},{10,11... | collective-permute-start | bytes 860168 | tf_op jit(solution)/shard_map/ppermute | solution.py:462
  16.9 1.9 %collective-permute-start.2 = (f32[70,8,128]{2,1,0:T(8,128)S(1)}, f32[70,8,128]{2,1,0:T(8,128)S(1)}, u32[]{:S(2)}, u32[]{:S(2)}) collective-permute-start(f32[70,8,128]{2,1,0:T(8,128)S(1)} %get-tuple-element.23), channel_id=1, source_target_pairs={{1,2},{2,1},{5,6},{6,5},{9,10},{10,9},{13,14},{14,13},{17,18},{18,... | collective-permute-start | bytes 860168 | tf_op jit(solution)/shard_map/ppermute | solution.py:461
  18.8 0.0 collective-permute-done.3.other
  18.9 0.7 %shard_map.52 = (f32[72,8,128]{2,1,0:T(8,128)S(1)}, f32[8,3072]{1,0:T(8,128)S(1)}, f32[24,8,128]{2,1,0:T(8,128)S(1)}) custom-call(f32[70,8,128]{2,1,0:T(8,128)S(1)} %collective-permute-done.3.other, f32[72,8,128]{2,1,0:T(8,128)S(1)} %get-tuple-element.28.pairs, f32[36,8,128]{2,1,0:T(8,128)S(1)} %get-tuple-element.29.base, f32[64,128]{1,0:T(8,128)S(1)} %get-tuple-element.26.rows), custom_call_target="tpu_custom_call" | custom-call | tf_op jit(solution)/shard_map/pallas_call | solution.py:51
  19.6 6.8 %collective-permute-done.2.other = f32[70,8,128]{2,1,0:T(8,128)S(1)} collective-permute-done((f32[70,8,128]{2,1,0:T(8,128)S(1)}, f32[70,8,128]{2,1,0:T(8,128)S(1)}, u32[]{:S(2)}, u32[]{:S(2)}) %collective-permute-start.2) | collective-permute-done | bytes 286752 | tf_op jit(solution)/shard_map/ppermute | solution.py:461
  26.4 1.6 %shard_map.53 = (f32[24,6144]{1,0:T(8,128)S(1)}, f32[32,2,128]{2,1,0:T(2,128)S(1)}) custom-call(f32[70,8,128]{2,1,0:T(8,128)S(1)} %collective-permute-done.2.other, f32[72,8,128]{2,1,0:T(8,128)S(1)} %get-tuple-element.24.pairs, f32[36,8,128]{2,1,0:T(8,128)S(1)} %get-tuple-element.25.base, f32[64,128]{1,0:T(8,128)S(1)} %get-tuple-element.26.rows, ...), custom_call_target="tpu_custom_call" | custom-call | tf_op jit(solution)/shard_map/pallas_call | solution.py:51
  28.0 19.6 %all_to_all.10.parts = f32[32,2,128]{2,1,0:T(2,128)S(1)} all-to-all(f32[32,2,128]{2,1,0:T(2,128)S(1)} %get-tuple-element.34), channel_id=1, replica_groups=mesh['tile_0'=4,'tile_1'=16,'tile_2'=2,'layer_0'=2,'layer_1'=2] {'tile_0..., dimensions={0} | all-to-all | bytes 65536 | tf_op jit(solution)/shard_map/all_to_all | solution.py:481
  47.7 20.6 %all_to_all.11.parts = f32[16,2,128]{2,1,0:T(2,128)S(1)} all-to-all(f32[16,2,128]{2,1,0:T(2,128)S(1)} %shard_map.54), channel_id=1, replica_groups=mesh['tile_0'=4,'tile_1'=16,'tile_2'=2,'layer_0'=2,'layer_1'=2] {'tile_1'}, dimensions={0} | all-to-all | bytes 32768 | tf_op jit(solution)/shard_map/all_to_all | solution.py:483
  68.2 2.5 %shard_map.55 = (f32[384,128]{1,0:T(8,128)}, f32[384,128]{1,0:T(8,128)}) custom-call(f32[16,2,128]{2,1,0:T(2,128)S(1)} %all_to_all.11.parts, f32[24,6144]{1,0:T(8,128)S(1)} %get-tuple-element.35.block), custom_call_target="tpu_custom_call" | custom-call | tf_op jit(solution)/shard_map/pallas_call | solution.py:51
  (1 shorter events, 0.0 us)
Async XLA Ops:
  1.7 5.5 %collective-permute-start = (f32[13,8,128]{2,1,0:T(8,128)S(1)}, f32[13,8,128]{2,1,0:T(8,128)S(1)}, u32[]{:S(2)}, u32[]{:S(2)}) collective-permute-start(f32[13,8,128]{2,1,0:T(8,128)S(1)} %get-tuple-element.21), channel_id=1, source_target_pairs={{0,4},{4,0},{8,12},{12,8},{16,20},{20,16},{24,28},{28,24},{32,36},... | collective-permute-start | bytes 159752 | tf_op jit(solution)/shard_map/ppermute | solution.py:445
  5.7 1.5 %collective-permute-start.1 = (f32[13,8,128]{2,1,0:T(8,128)S(1)}, f32[13,8,128]{2,1,0:T(8,128)S(1)}, u32[]{:S(2)}, u32[]{:S(2)}) collective-permute-start(f32[13,8,128]{2,1,0:T(8,128)S(1)} %get-tuple-element.22), channel_id=1, source_target_pairs={{4,8},{8,4},{12,16},{16,12},{20,24},{24,20},{28,32},{32,28},{36,40... | collective-permute-start | bytes 159752 | tf_op jit(solution)/shard_map/ppermute | solution.py:444
  7.7 11.2 %collective-permute-start.3 = (f32[70,8,128]{2,1,0:T(8,128)S(1)}, f32[70,8,128]{2,1,0:T(8,128)S(1)}, u32[]{:S(2)}, u32[]{:S(2)}) collective-permute-start(f32[70,8,128]{2,1,0:T(8,128)S(1)} %get-tuple-element.27), channel_id=1, source_target_pairs={{0,1},{1,0},{2,3},{3,2},{4,5},{5,4},{6,7},{7,6},{8,9},{9,8},{10,11... | collective-permute-start | bytes 860168 | tf_op jit(solution)/shard_map/ppermute | solution.py:462
  16.9 9.5 %collective-permute-start.2 = (f32[70,8,128]{2,1,0:T(8,128)S(1)}, f32[70,8,128]{2,1,0:T(8,128)S(1)}, u32[]{:S(2)}, u32[]{:S(2)}) collective-permute-start(f32[70,8,128]{2,1,0:T(8,128)S(1)} %get-tuple-element.23), channel_id=1, source_target_pairs={{1,2},{2,1},{5,6},{6,5},{9,10},{10,9},{13,14},{14,13},{17,18},{18,... | collective-permute-start | bytes 860168 | tf_op jit(solution)/shard_map/ppermute | solution.py:461

commit v5 on v4

--- a/solution.py
+++ b/solution.py
@@ -30,7 +30,7 @@
     return pltpu.VMEM((*shape, 8, SPAN), F32)
 
 
-def call(kernel, out_shape, scratch=(), smem=(), outside=()):
+def call(kernel, out_shape, scratch=(), smem=(), outside=(), aliases=None):
     def run(*args):
         specs = [
             pl.BlockSpec(memory_space=pltpu.SMEM if i in smem else pltpu.VMEM)
@@ -54,6 +54,7 @@
             in_specs=specs,
             out_specs=out_specs,
             scratch_shapes=list(scratch),
+            input_output_aliases=aliases or {},
         )(*args)
 
     return run
@@ -165,11 +166,14 @@
 
     def node(self, key, parts):
         ss, ds, sd, dd = parts
-        now_s, now_d = ss - ds, sd - dd
+        force = self.close(key, ss - ds, sd - dd)
+        self.left[key] = (ss + ds, sd + dd)
+        return force
+
+    def close(self, key, now_s, now_d):
         if key in self.left:
             now_s = now_s + self.left[key][0]
             now_d = now_d + self.left[key][1]
-        self.left[key] = (ss + ds, sd + dd)
         return (now_s - now_d) + pltpu.roll(now_s + now_d, 1, 1) * self.not_first
 
 
@@ -189,60 +193,163 @@
     return tuple(jnp.broadcast_to(rows[at : at + 1, :], (8, SPAN)) for at in (x, 16 + x))
 
 
+def pick(first_core, values):
+    return (
+        jnp.where(first_core, values[1], values[0]),
+        jnp.where(first_core, values[0], values[1]),
+    )
+
+
+def early_kernel(
+    own, pairs_a, pairs_b, base_a, base_b, to_a, to_b, rows, edge, norms
+):
+    first_core = lax.axis_index("layer_1") == 0
+    sign = jnp.where(first_core, -1.0, 1.0).astype(F32)
+    not_last, not_first = edge_masks()
+    for x in range(2, 10):
+        for c in range(3):
+            values = [own[(z * OWN_X + x - 2) * 3 + c] for z in range(OWN_Z)]
+            for to, pairs, value in zip(
+                (to_a, to_b), (pairs_a, pairs_b), pick(first_core, values)
+            ):
+                to[x * 3 + c] = value
+                pairs[(x * 3 + c) * 2], pairs[(x * 3 + c) * 2 + 1] = spread(value, not_last)
+    for z in range(OWN_Z):
+        for k in range(2):
+            at = (z * 2 + k) * 16
+            rows[at : at + 16, :] = jnp.zeros((16, SPAN), F32)
+            rows[at + 2 : at + 10, :] = own[48 + k * 2 + z]
+    column = Column(not_first)
+    for x in range(2, 9):
+        duals = element(layer_of(pairs_a, x, sign), layer_of(pairs_b, x, sign), *moduli(rows, x))
+        for c in range(3):
+            for side, parts in ((0, to_lower(duals, c)), (1, to_upper(duals, c))):
+                if x == 2:
+                    at = (side * 3 + c) * 2
+                    edge[at] = parts[0] - parts[1]
+                    edge[at + 1] = parts[2] - parts[3]
+                force = column.node((side, c), parts)
+                if x > 2:
+                    put(side, x, c, sign, force, (base_a, base_b), (to_a, to_b))
+    for side in range(2):
+        for c in range(3):
+            at = 12 + (side * 3 + c) * 2
+            edge[at], edge[at + 1] = column.left[side, c]
+    for to in (to_a, to_b):
+        for x in (0, 1, 10, 11):
+            for c in range(3):
+                to[x * 3 + c] = jnp.zeros((8, SPAN), F32)
+    every = jnp.concatenate([own[i] for i in range(2 * HALF)], 1)
+    gram = lax.dot_general(
+        every, every, (((1,), (1,)), ((), ())), precision=HIGHEST, preferred_element_type=F32
+    )
+    norms[...] = jnp.concatenate([gram, jnp.zeros((8, SPAN - 8), F32)], 1)
+
+
+def put(side, x, c, sign, force, bases, messages):
+    force = sign * force if c == 0 else force
+    bases[side][x * 3 + c] = force
+    messages[side][33 + x * 3 + c] = force
+
+
 def inner_kernel(
-    own, from_y, from_z, pairs_a, pairs_b, base_a, base_b, rows, to_a, to_b, probes_block
+    from_y,
+    from_z,
+    edge,
+    in_pairs_a,
+    in_pairs_b,
+    in_base_a,
+    in_base_b,
+    in_to_a,
+    in_to_b,
+    in_rows,
+    pairs_a,
+    pairs_b,
+    base_a,
+    base_b,
+    to_a,
+    to_b,
+    rows,
+    probes_block,
 ):
     odd = lax.axis_index("tile_2") == 1
     first_core = lax.axis_index("layer_1") == 0
     sign = jnp.where(first_core, -1.0, 1.0).astype(F32)
     not_last, not_first = edge_masks()
-    for x in range(WIDE_X):
+    for half, source in ((0, in_to_a), (1, in_to_b)):
+        for i in range(HALF):
+            at = (half * HALF + i) * SPAN
+            probes_block[:, at : at + SPAN] = source[6 + i]
+    fresh = {}
+    for x in (0, 1, 10, 11):
         for c in range(3):
             values = []
             for z in range(OWN_Z):
-                if x < 2:
-                    at = (z * 2 + x) * 3 + c
-                    values.append(jnp.where(odd, from_y[at], from_z[at]))
-                elif x < 10:
-                    values.append(own[(z * OWN_X + x - 2) * 3 + c])
-                else:
-                    at = (z * 2 + x - 10) * 3 + c
-                    values.append(jnp.where(odd, from_z[at], from_y[at]))
-            near_a = jnp.where(first_core, values[1], values[0])
-            near_b = jnp.where(first_core, values[0], values[1])
-            to_a[x * 3 + c] = near_a
-            to_b[x * 3 + c] = near_b
-            for half, pairs, value in ((0, pairs_a, near_a), (1, pairs_b, near_b)):
-                pairs[(x * 3 + c) * 2], pairs[(x * 3 + c) * 2 + 1] = spread(value, not_last)
-                if 2 <= x < 10:
-                    at = (half * HALF + (x - 2) * 3 + c) * SPAN
-                    probes_block[:, at : at + SPAN] = value
+                at = (z * 2 + x % 10) * 3 + c
+                one, two = from_y[at], from_z[at]
+                values.append(jnp.where(odd, one, two) if x < 2 else jnp.where(odd, two, one))
+            for side, to, pairs, value in zip(
+                (0, 1), (to_a, to_b), (pairs_a, pairs_b), pick(first_core, values)
+            ):
+                to[x * 3 + c] = value
+                fresh[side, x, c] = spread(value, not_last)
+                at = (x * 3 + c) * 2
+                pairs[at], pairs[at + 1] = fresh[side, x, c]
     left = jnp.where(odd, from_y[12], from_z[12])
     right = jnp.where(odd, from_z[12], from_y[12])
+    fields = {}
     for z in range(OWN_Z):
         for k in range(2):
             at = (z * 2 + k) * 16
-            rows[at + 2 : at + 10, :] = own[48 + k * 2 + z]
-            rows[at : at + 2, :] = left[k * 4 + z * 2 : k * 4 + z * 2 + 2]
-            rows[at + 10 : at + 12, :] = right[k * 4 + z * 2 : k * 4 + z * 2 + 2]
-            rows[at + 12 : at + 16, :] = jnp.zeros((4, SPAN), F32)
-    for i in range(4):
-        first, second = rows[i * 8 : i * 8 + 8, :], rows[32 + i * 8 : 40 + i * 8, :]
-        to_a[66 + i] = jnp.where(first_core, second, first)
-        to_b[66 + i] = jnp.where(first_core, first, second)
+            row = k * 4 + z * 2
+            rows[at : at + 2, :] = left[row : row + 2]
+            rows[at + 10 : at + 12, :] = right[row : row + 2]
+            whole = jnp.concatenate(
+                [left[row : row + 2], in_rows[at + 2 : at + 10, :], right[row : row + 2]]
+                + [jnp.zeros((4, SPAN), F32)],
+                0,
+            )
+            fields[z, k] = whole
+    for k in range(2):
+        for i in range(2):
+            one, two = pick(first_core, [fields[z, k][i * 8 : i * 8 + 8] for z in range(OWN_Z)])
+            to_a[66 + k * 2 + i] = one
+            to_b[66 + k * 2 + i] = two
+
+    def layer(side, x):
+        source = (in_pairs_a, in_pairs_b)[side]
+        combined = []
+        for c in range(3):
+            values = ()
+            for at in (x, x + 1):
+                if 2 <= at < 10:
+                    values += (source[(at * 3 + c) * 2], source[(at * 3 + c) * 2 + 1])
+                else:
+                    values += fresh[side, at, c]
+            if c == 0:
+                values = tuple(sign * value for value in values)
+            combined.append(along_x(values))
+        return combined
+
+    bases, messages = (base_a, base_b), (to_a, to_b)
     column = Column(not_first)
-    for x in range(WIDE_X - 1):
-        duals = element(layer_of(pairs_a, x, sign), layer_of(pairs_b, x, sign), *moduli(rows, x))
-        for c in range(3):
-            force_a = column.node((0, c), to_lower(duals, c))
-            force_b = column.node((1, c), to_upper(duals, c))
-            if x:
-                if c == 0:
-                    force_a, force_b = sign * force_a, sign * force_b
-                base_a[x * 3 + c] = force_a
-                base_b[x * 3 + c] = force_b
-                to_a[33 + x * 3 + c] = force_a
-                to_b[33 + x * 3 + c] = force_b
+    for x in (0, 1, 9, 10):
+        if x == 9:
+            for side in range(2):
+                for c in range(3):
+                    at = (side * 3 + c) * 2
+                    force = column.close((side, c), edge[at], edge[at + 1])
+                    put(side, 2, c, sign, force, bases, messages)
+                    column.left[side, c] = (edge[12 + at], edge[12 + at + 1])
+        lam, mu = (
+            jnp.broadcast_to(fields[0, k][x : x + 1], (8, SPAN)) for k in range(2)
+        )
+        duals = element(layer(0, x), layer(1, x), lam, mu)
+        for c in range(3):
+            for side, parts in ((0, to_lower(duals, c)), (1, to_upper(duals, c))):
+                force = column.node((side, c), parts)
+                if x:
+                    put(side, x, c, sign, force, bases, messages)
 
 
 def side_pass(above, other, pairs, base, rows, pairs_other, rows_side, near_one, far_one, one_block, first):
@@ -284,6 +391,14 @@
     return sign
 
 
+def thirds(values):
+    high = values.astype(jnp.bfloat16)
+    rest = values - high.astype(F32)
+    middle = rest.astype(jnp.bfloat16)
+    low = (rest - middle.astype(F32)).astype(jnp.bfloat16)
+    return high, middle, low
+
+
 def side_a_kernel(
     other, pairs, base, rows, near_one, one_block, two_side, pairs_other, rows_side, far_one
 ):
@@ -311,6 +426,7 @@
     one_block_a,
     two_a,
     probes_block,
+    norms,
     block,
     message,
     pairs_other,
@@ -343,14 +459,20 @@
                 block[16:24, at : at + SPAN] = force_a + two_a[(x - 2) * 3 + c]
                 at = at + HALF * SPAN
                 block[16:24, at : at + SPAN] = force_b
-    every = block[...]
-    grams = lax.dot_general(
-        every[0:16], every, (((1,), (1,)), ((), ())), precision=HIGHEST, preferred_element_type=F32
-    )
+    left = jnp.concatenate(thirds(block[0:16, :]), 0)
+    right = jnp.concatenate(thirds(block[8:24, :]), 0)
+    products = lax.dot_general(
+        left, right, (((1,), (1,)), ((), ())), preferred_element_type=F32
+    )
+    grams = None
+    for one in (2, 1, 0):
+        for two in range(2 - one, -1, -1):
+            term = products[one * 16 : one * 16 + 16, two * 16 : two * 16 + 16]
+            grams = term if grams is None else grams + term
     lanes = lax.broadcasted_iota(jnp.int32, (8, SPAN), 1)
-    wide = jnp.concatenate([grams, jnp.zeros((16, SPAN - 24), F32)], 1)
-    packed = jnp.where(lanes < 16, wide[0:8], pltpu.roll(wide[8:16], 8, 1))
-    packed = turned(jnp.where(lanes < 32, packed, 0.0), 1)
+    wide = jnp.concatenate([grams, jnp.zeros((16, SPAN - 16), F32)], 1)
+    packed = jnp.where(lanes < 16, pltpu.roll(wide[0:8], 8, 1), pltpu.roll(wide[8:16], 16, 1))
+    packed = turned(jnp.where(lanes < 8, norms[...], packed), 1)
     halves = [packed[i : i + 1] + packed[i + 1 : i + 2] for i in (0, 2, 4, 6)]
     packed = jnp.concatenate([halves[0] + halves[1], halves[2] + halves[3]], 0)
     for i in range(message.shape[0]):
@@ -375,11 +497,13 @@
 
 def eliminate(table, first):
     rows = lax.broadcasted_iota(jnp.int32, (8, SPAN), 0)
+    lanes = lax.broadcasted_iota(jnp.int32, (8, SPAN), 1)
+    nothing = jnp.where(lanes < 0, 1.0, 0.0).astype(F32)
     for k in range(0, 8, 2):
         top = jnp.broadcast_to(table[k : k + 1, :], (8, SPAN))
         low = jnp.broadcast_to(table[k + 1 : k + 2, :], (8, SPAN))
-        left = jnp.broadcast_to(table[:, first + k : first + k + 1], (8, SPAN))
-        right = jnp.broadcast_to(table[:, first + k + 1 : first + k + 2], (8, SPAN))
+        left = jnp.broadcast_to(table[:, first + k : first + k + 1], (8, SPAN)) + nothing
+        right = jnp.broadcast_to(table[:, first + k + 1 : first + k + 2], (8, SPAN)) + nothing
         p00 = jnp.broadcast_to(left[k : k + 1, :], (8, SPAN))
         p10 = jnp.broadcast_to(left[k + 1 : k + 2, :], (8, SPAN))
         p01 = jnp.broadcast_to(right[k : k + 1, :], (8, SPAN))
@@ -441,23 +565,32 @@
     own, to_y, to_z = call(pack_kernel, (vregs(52), vregs(EDGE), vregs(EDGE)), smem=(0,), outside=(1, 2))(
         lame_pairs.T, probes.reshape(PROBES * ROWS, SPAN), material
     )
+    moduli_rows = pltpu.VMEM((64, SPAN), F32)
+    shared = (
+        vregs(SIDE),
+        vregs(SIDE),
+        vregs(36),
+        vregs(36),
+        vregs(FULL),
+        vregs(FULL),
+        moduli_rows,
+    )
+    *arrays, edge, norms = call(
+        early_kernel,
+        (
+            *shared,
+            vregs(24),
+            pltpu.VMEM((8, SPAN), F32),
+        ),
+    )(own)
     from_z = lax.ppermute(to_z, TILE, in_z)
     from_y = lax.ppermute(to_y, TILE, in_y)
-    moduli_rows = pltpu.VMEM((64, SPAN), F32)
+    pairs_a, pairs_b, base_a, base_b, to_a, to_b, rows, probes_block = call(
+        inner_kernel,
+        (*shared, pltpu.VMEM((8, 2 * HALF * SPAN), F32)),
+        aliases={3 + i: i for i in range(7)},
+    )(from_y, from_z, edge, *arrays)
     half_block = pltpu.VMEM((8, HALF * SPAN), F32)
-    pairs_a, pairs_b, base_a, base_b, rows, to_a, to_b, probes_block = call(
-        inner_kernel,
-        (
-            vregs(SIDE),
-            vregs(SIDE),
-            vregs(36),
-            vregs(36),
-            moduli_rows,
-            vregs(FULL),
-            vregs(FULL),
-            pltpu.VMEM((8, 2 * HALF * SPAN), F32),
-        ),
-    )(own, from_y, from_z)
     from_b = lax.ppermute(to_b, LAYER, in_chip)
     from_a = lax.ppermute(to_a, LAYER, in_core)
     planes = lax.axis_size(PLANE)
@@ -477,7 +610,7 @@
             pltpu.VMEM((SIDE, 8, SPAN), F32),
             half_block,
         ),
-    )(from_b, pairs_b, base_b, rows, near_a, one_block_a, two_a, probes_block)
+    )(from_b, pairs_b, base_b, rows, near_a, one_block_a, two_a, probes_block, norms)
     parts = lax.all_to_all(message, PLANE, 0, 0, tiled=True)
     message = call(total_kernel, pltpu.VMEM((columns, 2, SPAN), F32))(parts)
     parts = lax.all_to_all(message, COLUMN, 0, 0, tiled=True)

time: 71 us -> 70.3 us (level)
    pallas_call x6 -> x7, Pallas kernels: 6.38 us -> 6.22 us  [run(): pl.pallas_call(kernel, out_shape=out_shape, in_specs=specs, out_specs=out...]
  transfers between devices with their start and end apart: 4 -> 4, of which waited for: 2 -> 2; matrix products, arithmetic and copies ran while one was open for 0% -> 0% of each run, Pallas kernels for 1% -> 2%
where the time goes in v5:
time: 70.3 us; the launch traced here: 70 us
  blocking collectives  40.2 us (57%)
  starting transfers between devices  15.8 us (22%)
  waiting for transfers between devices  7.05 us (10%)
  Pallas kernels  6.22 us (9%)
    all_to_all x1, blocking collectives, body(): parts = lax.all_to_all(message, COLUMN, 0, 0, tiled=True)  20.6 us
    all_to_all x1, blocking collectives, body(): parts = lax.all_to_all(message, PLANE, 0, 0, tiled=True)  19.6 us
    ppermute x1, starting transfers between devices, body(): from_a = lax.ppermute(to_a, LAYER, in_core)  9.24 us
    ppermute x1, waiting for transfers between devices, body(): from_b = lax.ppermute(to_b, LAYER, in_chip)  6.8 us
    pallas_call x7, Pallas kernels, run(): pl.pallas_call(kernel, out_shape=out_shape, in_specs=specs, out_specs=out...  6.22 us
    ppermute x1, starting transfers between devices, body(): from_y = lax.ppermute(to_y, TILE, in_y)  4.02 us
    ppermute x1, starting transfers between devices, body(): from_b = lax.ppermute(to_b, LAYER, in_chip)  1.92 us
  transfers between devices with their start and end apart: 4, of which 2 were waited for; matrix products, arithmetic and copies ran while one was open for 0% of the time, Pallas kernels for 2%

profile of v5, /device:TPU:1, one launch (start us, length us, event | category | flops | bytes accessed | tf_op | source)
XLA Modules:
  0.0 70.0 jit_solution(13582152509216645867)
XLA Ops:
  0.6 1.0 %shard_map.50 = (f32[52,8,128]{2,1,0:T(8,128)S(1)}, f32[13,8,128]{2,1,0:T(8,128)S(1)}, f32[13,8,128]{2,1,0:T(8,128)S(1)}) custom-call(f32[2,3]{1,0:T(2,128)} %bitcast.5, f32[384,128]{1,0:T(8,128)} %bitcast.4, s32[2,8,128]{2,1,0:T(8,128)} %material.1), custom_call_target="tpu_custom_call" | custom-call | tf_op jit(solution)/shard_map/pallas_call | solution.py:51
  1.7 4.0 %collective-permute-start = (f32[13,8,128]{2,1,0:T(8,128)S(1)}, f32[13,8,128]{2,1,0:T(8,128)S(1)}, u32[]{:S(2)}, u32[]{:S(2)}) collective-permute-start(f32[13,8,128]{2,1,0:T(8,128)S(1)} %get-tuple-element.29), channel_id=1, source_target_pairs={{0,4},{4,0},{8,12},{12,8},{16,20},{20,16},{24,28},{28,24},{32,36},... | collective-permute-start | bytes 159752 | tf_op jit(solution)/shard_map/ppermute | solution.py:587
  5.7 0.7 collective-permute-start.1
  6.4 0.6 shard_map.51
  6.9 0.2 collective-permute-done.from_y
  7.2 0.0 collective-permute-done.1.from_z
  7.2 0.3 shard_map.52
  7.4 9.2 %collective-permute-start.3 = (f32[70,8,128]{2,1,0:T(8,128)S(1)}, f32[70,8,128]{2,1,0:T(8,128)S(1)}, u32[]{:S(2)}, u32[]{:S(2)}) collective-permute-start(f32[70,8,128]{2,1,0:T(8,128)S(1)} %get-tuple-element.44), channel_id=1, source_target_pairs={{0,1},{1,0},{2,3},{3,2},{4,5},{5,4},{6,7},{7,6},{8,9},{9,8},{10,11... | collective-permute-start | bytes 860168 | tf_op jit(solution)/shard_map/ppermute | solution.py:595
  16.7 1.9 %collective-permute-start.2 = (f32[70,8,128]{2,1,0:T(8,128)S(1)}, f32[70,8,128]{2,1,0:T(8,128)S(1)}, u32[]{:S(2)}, u32[]{:S(2)}) collective-permute-start(f32[70,8,128]{2,1,0:T(8,128)S(1)} %get-tuple-element.40), channel_id=1, source_target_pairs={{1,2},{2,1},{5,6},{6,5},{9,10},{10,9},{13,14},{14,13},{17,18},{18,... | collective-permute-start | bytes 860168 | tf_op jit(solution)/shard_map/ppermute | solution.py:594
  18.6 0.0 collective-permute-done.3.other
  18.6 0.7 %shard_map.53 = (f32[72,8,128]{2,1,0:T(8,128)S(1)}, f32[8,3072]{1,0:T(8,128)S(1)}, f32[24,8,128]{2,1,0:T(8,128)S(1)}) custom-call(f32[70,8,128]{2,1,0:T(8,128)S(1)} %collective-permute-done.3.other, f32[72,8,128]{2,1,0:T(8,128)S(1)} %get-tuple-element.45.pairs, f32[36,8,128]{2,1,0:T(8,128)S(1)} %get-tuple-element.46.base, f32[64,128]{1,0:T(8,128)S(1)} %get-tuple-element.43.rows), custom_call_target="tpu_custom_call" | custom-call | tf_op jit(solution)/shard_map/pallas_call | solution.py:51
  19.4 6.8 %collective-permute-done.2.other = f32[70,8,128]{2,1,0:T(8,128)S(1)} collective-permute-done((f32[70,8,128]{2,1,0:T(8,128)S(1)}, f32[70,8,128]{2,1,0:T(8,128)S(1)}, u32[]{:S(2)}, u32[]{:S(2)}) %collective-permute-start.2) | collective-permute-done | bytes 286752 | tf_op jit(solution)/shard_map/ppermute | solution.py:594
  26.2 1.4 %shard_map.54 = (f32[24,6144]{1,0:T(8,128)S(1)}, f32[32,2,128]{2,1,0:T(2,128)S(1)}) custom-call(f32[70,8,128]{2,1,0:T(8,128)S(1)} %collective-permute-done.2.other, f32[72,8,128]{2,1,0:T(8,128)S(1)} %get-tuple-element.41.pairs, f32[36,8,128]{2,1,0:T(8,128)S(1)} %get-tuple-element.42.base, f32[64,128]{1,0:T(8,128)S(1)} %get-tuple-element.43.rows, ...), custom_call_target="tpu_custom_call" | custom-call | tf_op jit(solution)/shard_map/pallas_call | solution.py:51
  27.5 19.6 %all_to_all.10.parts = f32[32,2,128]{2,1,0:T(2,128)S(1)} all-to-all(f32[32,2,128]{2,1,0:T(2,128)S(1)} %get-tuple-element.52), channel_id=1, replica_groups=mesh['tile_0'=4,'tile_1'=16,'tile_2'=2,'layer_0'=2,'layer_1'=2] {'tile_0..., dimensions={0} | all-to-all | bytes 65536 | tf_op jit(solution)/shard_map/all_to_all | solution.py:614
  47.2 20.6 %all_to_all.11.parts = f32[16,2,128]{2,1,0:T(2,128)S(1)} all-to-all(f32[16,2,128]{2,1,0:T(2,128)S(1)} %shard_map.55), channel_id=1, replica_groups=mesh['tile_0'=4,'tile_1'=16,'tile_2'=2,'layer_0'=2,'layer_1'=2] {'tile_1'}, dimensions={0} | all-to-all | bytes 32768 | tf_op jit(solution)/shard_map/all_to_all | solution.py:616
  67.8 2.2 %shard_map.56 = (f32[384,128]{1,0:T(8,128)}, f32[384,128]{1,0:T(8,128)}) custom-call(f32[16,2,128]{2,1,0:T(2,128)S(1)} %all_to_all.11.parts, f32[24,6144]{1,0:T(8,128)S(1)} %get-tuple-element.53.block), custom_call_target="tpu_custom_call" | custom-call | tf_op jit(solution)/shard_map/pallas_call | solution.py:51
  (1 shorter events, 0.0 us)
Async XLA Ops:
  1.7 5.5 %collective-permute-start = (f32[13,8,128]{2,1,0:T(8,128)S(1)}, f32[13,8,128]{2,1,0:T(8,128)S(1)}, u32[]{:S(2)}, u32[]{:S(2)}) collective-permute-start(f32[13,8,128]{2,1,0:T(8,128)S(1)} %get-tuple-element.29), channel_id=1, source_target_pairs={{0,4},{4,0},{8,12},{12,8},{16,20},{20,16},{24,28},{28,24},{32,36},... | collective-permute-start | bytes 159752 | tf_op jit(solution)/shard_map/ppermute | solution.py:587
  5.7 1.5 %collective-permute-start.1 = (f32[13,8,128]{2,1,0:T(8,128)S(1)}, f32[13,8,128]{2,1,0:T(8,128)S(1)}, u32[]{:S(2)}, u32[]{:S(2)}) collective-permute-start(f32[13,8,128]{2,1,0:T(8,128)S(1)} %get-tuple-element.30), channel_id=1, source_target_pairs={{4,8},{8,4},{12,16},{16,12},{20,24},{24,20},{28,32},{32,28},{36,40... | collective-permute-start | bytes 159752 | tf_op jit(solution)/shard_map/ppermute | solution.py:586
  7.4 11.2 %collective-permute-start.3 = (f32[70,8,128]{2,1,0:T(8,128)S(1)}, f32[70,8,128]{2,1,0:T(8,128)S(1)}, u32[]{:S(2)}, u32[]{:S(2)}) collective-permute-start(f32[70,8,128]{2,1,0:T(8,128)S(1)} %get-tuple-element.44), channel_id=1, source_target_pairs={{0,1},{1,0},{2,3},{3,2},{4,5},{5,4},{6,7},{7,6},{8,9},{9,8},{10,11... | collective-permute-start | bytes 860168 | tf_op jit(solution)/shard_map/ppermute | solution.py:595
  16.7 9.5 %collective-permute-start.2 = (f32[70,8,128]{2,1,0:T(8,128)S(1)}, f32[70,8,128]{2,1,0:T(8,128)S(1)}, u32[]{:S(2)}, u32[]{:S(2)}) collective-permute-start(f32[70,8,128]{2,1,0:T(8,128)S(1)} %get-tuple-element.40), channel_id=1, source_target_pairs={{1,2},{2,1},{5,6},{6,5},{9,10},{10,9},{13,14},{14,13},{17,18},{18,... | collective-permute-start | bytes 860168 | tf_op jit(solution)/shard_map/ppermute | solution.py:594

commit v6 on v5

--- a/solution.py
+++ b/solution.py
@@ -9,7 +9,7 @@
 
 TILE = ("tile_0", "tile_1", "tile_2")
 LAYER = ("layer_0", "layer_1")
-PLANE = ("tile_0", "tile_2", "layer_0", "layer_1")
+PLANE = ("layer_1", "tile_0", "tile_2", "layer_0")
 COLUMN = "tile_1"
 
 PROBES = 8
@@ -542,8 +542,15 @@
         [coef_b, -coef_c - pltpu.roll(coef_b, 8, 1), pltpu.roll(coef_c, 8, 1)], 0
     )[:, 0:16]
     every = block[...]
+    ones, twos = (
+        jnp.concatenate([parts_of[i].astype(F32) for i in order], 0).astype(jnp.bfloat16)
+        for parts_of, order in (
+            (thirds(coefs), (2, 1, 0, 1, 0, 0)),
+            (thirds(every), (0, 1, 2, 0, 1, 0)),
+        )
+    )
     mixed = lax.dot_general(
-        coefs, every, (((0,), (0,)), ((), ())), precision=HIGHEST, preferred_element_type=F32
+        ones, twos, (((0,), (0,)), ((), ())), preferred_element_type=F32
     )
     first_core = lax.axis_index("layer_1") == 0
     for half in range(2):

time: 70.3 us -> 69.8 us (level)
  no operation moved by 1% of the time
where the time goes in v6:
time: 69.8 us; the launch traced here: 69.6 us
  blocking collectives  40 us (57%)
  starting transfers between devices  15.8 us (23%)
  waiting for transfers between devices  7.05 us (10%)
  Pallas kernels  5.97 us (9%)
  between operations  0.7 us (1%)
    all_to_all x1, blocking collectives, body(): parts = lax.all_to_all(message, COLUMN, 0, 0, tiled=True)  20.6 us
    all_to_all x1, blocking collectives, body(): parts = lax.all_to_all(message, PLANE, 0, 0, tiled=True)  19.4 us
    ppermute x1, starting transfers between devices, body(): from_a = lax.ppermute(to_a, LAYER, in_core)  9.24 us
    ppermute x1, waiting for transfers between devices, body(): from_b = lax.ppermute(to_b, LAYER, in_chip)  6.8 us
    pallas_call x7, Pallas kernels, run(): pl.pallas_call(kernel, out_shape=out_shape, in_specs=specs, out_specs=out...  5.97 us
    ppermute x1, starting transfers between devices, body(): from_y = lax.ppermute(to_y, TILE, in_y)  4.02 us
    ppermute x1, starting transfers between devices, body(): from_b = lax.ppermute(to_b, LAYER, in_chip)  1.92 us
  transfers between devices with their start and end apart: 4, of which 2 were waited for; matrix products, arithmetic and copies ran while one was open for 0% of the time, Pallas kernels for 2%

profile of v6, /device:TPU:1, one launch (start us, length us, event | category | flops | bytes accessed | tf_op | source)
XLA Modules:
  0.0 69.6 jit_solution(5344545130132242559)
XLA Ops:
  0.6 1.0 %shard_map.50 = (f32[52,8,128]{2,1,0:T(8,128)S(1)}, f32[13,8,128]{2,1,0:T(8,128)S(1)}, f32[13,8,128]{2,1,0:T(8,128)S(1)}) custom-call(f32[2,3]{1,0:T(2,128)} %bitcast.5, f32[384,128]{1,0:T(8,128)} %bitcast.4, s32[2,8,128]{2,1,0:T(8,128)} %material.1), custom_call_target="tpu_custom_call" | custom-call | tf_op jit(solution)/shard_map/pallas_call | solution.py:51
  1.7 4.0 %collective-permute-start = (f32[13,8,128]{2,1,0:T(8,128)S(1)}, f32[13,8,128]{2,1,0:T(8,128)S(1)}, u32[]{:S(2)}, u32[]{:S(2)}) collective-permute-start(f32[13,8,128]{2,1,0:T(8,128)S(1)} %get-tuple-element.29), channel_id=1, source_target_pairs={{0,4},{4,0},{8,12},{12,8},{16,20},{20,16},{24,28},{28,24},{32,36},... | collective-permute-start | bytes 159752 | tf_op jit(solution)/shard_map/ppermute | solution.py:594
  5.7 0.7 collective-permute-start.1
  6.4 0.6 shard_map.51
  6.9 0.2 collective-permute-done.from_y
  7.2 0.0 collective-permute-done.1.from_z
  7.2 0.3 shard_map.52
  7.4 9.2 %collective-permute-start.3 = (f32[70,8,128]{2,1,0:T(8,128)S(1)}, f32[70,8,128]{2,1,0:T(8,128)S(1)}, u32[]{:S(2)}, u32[]{:S(2)}) collective-permute-start(f32[70,8,128]{2,1,0:T(8,128)S(1)} %get-tuple-element.44), channel_id=1, source_target_pairs={{0,1},{1,0},{2,3},{3,2},{4,5},{5,4},{6,7},{7,6},{8,9},{9,8},{10,11... | collective-permute-start | bytes 860168 | tf_op jit(solution)/shard_map/ppermute | solution.py:602
  16.7 1.9 %collective-permute-start.2 = (f32[70,8,128]{2,1,0:T(8,128)S(1)}, f32[70,8,128]{2,1,0:T(8,128)S(1)}, u32[]{:S(2)}, u32[]{:S(2)}) collective-permute-start(f32[70,8,128]{2,1,0:T(8,128)S(1)} %get-tuple-element.40), channel_id=1, source_target_pairs={{1,2},{2,1},{5,6},{6,5},{9,10},{10,9},{13,14},{14,13},{17,18},{18,... | collective-permute-start | bytes 860168 | tf_op jit(solution)/shard_map/ppermute | solution.py:601
  18.6 0.0 collective-permute-done.3.other
  18.6 0.7 %shard_map.53 = (f32[72,8,128]{2,1,0:T(8,128)S(1)}, f32[8,3072]{1,0:T(8,128)S(1)}, f32[24,8,128]{2,1,0:T(8,128)S(1)}) custom-call(f32[70,8,128]{2,1,0:T(8,128)S(1)} %collective-permute-done.3.other, f32[72,8,128]{2,1,0:T(8,128)S(1)} %get-tuple-element.45.pairs, f32[36,8,128]{2,1,0:T(8,128)S(1)} %get-tuple-element.46.base, f32[64,128]{1,0:T(8,128)S(1)} %get-tuple-element.43.rows), custom_call_target="tpu_custom_call" | custom-call | tf_op jit(solution)/shard_map/pallas_call | solution.py:51
  19.4 6.8 %collective-permute-done.2.other = f32[70,8,128]{2,1,0:T(8,128)S(1)} collective-permute-done((f32[70,8,128]{2,1,0:T(8,128)S(1)}, f32[70,8,128]{2,1,0:T(8,128)S(1)}, u32[]{:S(2)}, u32[]{:S(2)}) %collective-permute-start.2) | collective-permute-done | bytes 286752 | tf_op jit(solution)/shard_map/ppermute | solution.py:601
  26.2 1.4 %shard_map.54 = (f32[24,6144]{1,0:T(8,128)S(1)}, f32[32,2,128]{2,1,0:T(2,128)S(1)}) custom-call(f32[70,8,128]{2,1,0:T(8,128)S(1)} %collective-permute-done.2.other, f32[72,8,128]{2,1,0:T(8,128)S(1)} %get-tuple-element.41.pairs, f32[36,8,128]{2,1,0:T(8,128)S(1)} %get-tuple-element.42.base, f32[64,128]{1,0:T(8,128)S(1)} %get-tuple-element.43.rows, ...), custom_call_target="tpu_custom_call" | custom-call | tf_op jit(solution)/shard_map/pallas_call | solution.py:51
  27.5 19.4 %all_to_all.10.parts = f32[32,2,128]{2,1,0:T(2,128)S(1)} all-to-all(f32[32,2,128]{2,1,0:T(2,128)S(1)} %get-tuple-element.52), channel_id=1, replica_groups=mesh['tile_0'=4,'tile_1'=16,'tile_2'=2,'layer_0'=2,'layer_1'=2] {'layer_..., dimensions={0} | all-to-all | bytes 65536 | tf_op jit(solution)/shard_map/all_to_all | solution.py:621
  47.0 20.6 %all_to_all.11.parts = f32[16,2,128]{2,1,0:T(2,128)S(1)} all-to-all(f32[16,2,128]{2,1,0:T(2,128)S(1)} %shard_map.55), channel_id=1, replica_groups=mesh['tile_0'=4,'tile_1'=16,'tile_2'=2,'layer_0'=2,'layer_1'=2] {'tile_1'}, dimensions={0} | all-to-all | bytes 32768 | tf_op jit(solution)/shard_map/all_to_all | solution.py:623
  67.6 2.0 %shard_map.56 = (f32[384,128]{1,0:T(8,128)}, f32[384,128]{1,0:T(8,128)}) custom-call(f32[16,2,128]{2,1,0:T(2,128)S(1)} %all_to_all.11.parts, f32[24,6144]{1,0:T(8,128)S(1)} %get-tuple-element.53.block), custom_call_target="tpu_custom_call" | custom-call | tf_op jit(solution)/shard_map/pallas_call | solution.py:51
  (1 shorter events, 0.0 us)
Async XLA Ops:
  1.7 5.5 %collective-permute-start = (f32[13,8,128]{2,1,0:T(8,128)S(1)}, f32[13,8,128]{2,1,0:T(8,128)S(1)}, u32[]{:S(2)}, u32[]{:S(2)}) collective-permute-start(f32[13,8,128]{2,1,0:T(8,128)S(1)} %get-tuple-element.29), channel_id=1, source_target_pairs={{0,4},{4,0},{8,12},{12,8},{16,20},{20,16},{24,28},{28,24},{32,36},... | collective-permute-start | bytes 159752 | tf_op jit(solution)/shard_map/ppermute | solution.py:594
  5.7 1.5 %collective-permute-start.1 = (f32[13,8,128]{2,1,0:T(8,128)S(1)}, f32[13,8,128]{2,1,0:T(8,128)S(1)}, u32[]{:S(2)}, u32[]{:S(2)}) collective-permute-start(f32[13,8,128]{2,1,0:T(8,128)S(1)} %get-tuple-element.30), channel_id=1, source_target_pairs={{4,8},{8,4},{12,16},{16,12},{20,24},{24,20},{28,32},{32,28},{36,40... | collective-permute-start | bytes 159752 | tf_op jit(solution)/shard_map/ppermute | solution.py:593
  7.4 11.2 %collective-permute-start.3 = (f32[70,8,128]{2,1,0:T(8,128)S(1)}, f32[70,8,128]{2,1,0:T(8,128)S(1)}, u32[]{:S(2)}, u32[]{:S(2)}) collective-permute-start(f32[70,8,128]{2,1,0:T(8,128)S(1)} %get-tuple-element.44), channel_id=1, source_target_pairs={{0,1},{1,0},{2,3},{3,2},{4,5},{5,4},{6,7},{7,6},{8,9},{9,8},{10,11... | collective-permute-start | bytes 860168 | tf_op jit(solution)/shard_map/ppermute | solution.py:602
  16.7 9.5 %collective-permute-start.2 = (f32[70,8,128]{2,1,0:T(8,128)S(1)}, f32[70,8,128]{2,1,0:T(8,128)S(1)}, u32[]{:S(2)}, u32[]{:S(2)}) collective-permute-start(f32[70,8,128]{2,1,0:T(8,128)S(1)} %get-tuple-element.40), channel_id=1, source_target_pairs={{1,2},{2,1},{5,6},{6,5},{9,10},{10,9},{13,14},{14,13},{17,18},{18,... | collective-permute-start | bytes 860168 | tf_op jit(solution)/shard_map/ppermute | solution.py:601

commit v7 on v6

--- a/solution.py
+++ b/solution.py
@@ -459,8 +459,9 @@
                 block[16:24, at : at + SPAN] = force_a + two_a[(x - 2) * 3 + c]
                 at = at + HALF * SPAN
                 block[16:24, at : at + SPAN] = force_b
-    left = jnp.concatenate(thirds(block[0:16, :]), 0)
-    right = jnp.concatenate(thirds(block[8:24, :]), 0)
+    split = [part.astype(F32) for part in thirds(block[...])]
+    left = jnp.concatenate([part[0:16] for part in split], 0).astype(jnp.bfloat16)
+    right = jnp.concatenate([part[8:24] for part in split], 0).astype(jnp.bfloat16)
     products = lax.dot_general(
         left, right, (((1,), (1,)), ((), ())), preferred_element_type=F32
     )

time: 69.8 us -> 69.8 us (level)
  no operation moved by 1% of the time
where the time goes in v7:
time: 69.8 us; the launch traced here: 69.6 us
  blocking collectives  40 us (57%)
  starting transfers between devices  15.8 us (23%)
  waiting for transfers between devices  7.05 us (10%)
  Pallas kernels  5.97 us (9%)
  between operations  0.7 us (1%)
    all_to_all x1, blocking collectives, body(): parts = lax.all_to_all(message, COLUMN, 0, 0, tiled=True)  20.6 us
    all_to_all x1, blocking collectives, body(): parts = lax.all_to_all(message, PLANE, 0, 0, tiled=True)  19.4 us
    ppermute x1, starting transfers between devices, body(): from_a = lax.ppermute(to_a, LAYER, in_core)  9.24 us
    ppermute x1, waiting for transfers between devices, body(): from_b = lax.ppermute(to_b, LAYER, in_chip)  6.8 us
    pallas_call x7, Pallas kernels, run(): pl.pallas_call(kernel, out_shape=out_shape, in_specs=specs, out_specs=out...  5.97 us
    ppermute x1, starting transfers between devices, body(): from_y = lax.ppermute(to_y, TILE, in_y)  4.02 us
    ppermute x1, starting transfers between devices, body(): from_b = lax.ppermute(to_b, LAYER, in_chip)  1.92 us
  transfers between devices with their start and end apart: 4, of which 2 were waited for; matrix products, arithmetic and copies ran while one was open for 0% of the time, Pallas kernels for 2%

profile of v7, /device:TPU:1, one launch (start us, length us, event | category | flops | bytes accessed | tf_op | source)
XLA Modules:
  0.0 69.6 jit_solution(12743906081052342355)
XLA Ops:
  0.6 1.0 %shard_map.50 = (f32[52,8,128]{2,1,0:T(8,128)S(1)}, f32[13,8,128]{2,1,0:T(8,128)S(1)}, f32[13,8,128]{2,1,0:T(8,128)S(1)}) custom-call(f32[2,3]{1,0:T(2,128)} %bitcast.5, f32[384,128]{1,0:T(8,128)} %bitcast.4, s32[2,8,128]{2,1,0:T(8,128)} %material.1), custom_call_target="tpu_custom_call" | custom-call | tf_op jit(solution)/shard_map/pallas_call | solution.py:51
  1.7 4.0 %collective-permute-start = (f32[13,8,128]{2,1,0:T(8,128)S(1)}, f32[13,8,128]{2,1,0:T(8,128)S(1)}, u32[]{:S(2)}, u32[]{:S(2)}) collective-permute-start(f32[13,8,128]{2,1,0:T(8,128)S(1)} %get-tuple-element.29), channel_id=1, source_target_pairs={{0,4},{4,0},{8,12},{12,8},{16,20},{20,16},{24,28},{28,24},{32,36},... | collective-permute-start | bytes 159752 | tf_op jit(solution)/shard_map/ppermute | solution.py:595
  5.7 0.7 collective-permute-start.1
  6.4 0.6 shard_map.51
  6.9 0.2 collective-permute-done.from_y
  7.2 0.0 collective-permute-done.1.from_z
  7.2 0.3 shard_map.52
  7.4 9.2 %collective-permute-start.3 = (f32[70,8,128]{2,1,0:T(8,128)S(1)}, f32[70,8,128]{2,1,0:T(8,128)S(1)}, u32[]{:S(2)}, u32[]{:S(2)}) collective-permute-start(f32[70,8,128]{2,1,0:T(8,128)S(1)} %get-tuple-element.44), channel_id=1, source_target_pairs={{0,1},{1,0},{2,3},{3,2},{4,5},{5,4},{6,7},{7,6},{8,9},{9,8},{10,11... | collective-permute-start | bytes 860168 | tf_op jit(solution)/shard_map/ppermute | solution.py:603
  16.7 1.9 %collective-permute-start.2 = (f32[70,8,128]{2,1,0:T(8,128)S(1)}, f32[70,8,128]{2,1,0:T(8,128)S(1)}, u32[]{:S(2)}, u32[]{:S(2)}) collective-permute-start(f32[70,8,128]{2,1,0:T(8,128)S(1)} %get-tuple-element.40), channel_id=1, source_target_pairs={{1,2},{2,1},{5,6},{6,5},{9,10},{10,9},{13,14},{14,13},{17,18},{18,... | collective-permute-start | bytes 860168 | tf_op jit(solution)/shard_map/ppermute | solution.py:602
  18.6 0.0 collective-permute-done.3.other
  18.6 0.7 %shard_map.53 = (f32[72,8,128]{2,1,0:T(8,128)S(1)}, f32[8,3072]{1,0:T(8,128)S(1)}, f32[24,8,128]{2,1,0:T(8,128)S(1)}) custom-call(f32[70,8,128]{2,1,0:T(8,128)S(1)} %collective-permute-done.3.other, f32[72,8,128]{2,1,0:T(8,128)S(1)} %get-tuple-element.45.pairs, f32[36,8,128]{2,1,0:T(8,128)S(1)} %get-tuple-element.46.base, f32[64,128]{1,0:T(8,128)S(1)} %get-tuple-element.43.rows), custom_call_target="tpu_custom_call" | custom-call | tf_op jit(solution)/shard_map/pallas_call | solution.py:51
  19.4 6.8 %collective-permute-done.2.other = f32[70,8,128]{2,1,0:T(8,128)S(1)} collective-permute-done((f32[70,8,128]{2,1,0:T(8,128)S(1)}, f32[70,8,128]{2,1,0:T(8,128)S(1)}, u32[]{:S(2)}, u32[]{:S(2)}) %collective-permute-start.2) | collective-permute-done | bytes 286752 | tf_op jit(solution)/shard_map/ppermute | solution.py:602
  26.2 1.4 %shard_map.54 = (f32[24,6144]{1,0:T(8,128)S(1)}, f32[32,2,128]{2,1,0:T(2,128)S(1)}) custom-call(f32[70,8,128]{2,1,0:T(8,128)S(1)} %collective-permute-done.2.other, f32[72,8,128]{2,1,0:T(8,128)S(1)} %get-tuple-element.41.pairs, f32[36,8,128]{2,1,0:T(8,128)S(1)} %get-tuple-element.42.base, f32[64,128]{1,0:T(8,128)S(1)} %get-tuple-element.43.rows, ...), custom_call_target="tpu_custom_call" | custom-call | tf_op jit(solution)/shard_map/pallas_call | solution.py:51
  27.5 19.4 %all_to_all.10.parts = f32[32,2,128]{2,1,0:T(2,128)S(1)} all-to-all(f32[32,2,128]{2,1,0:T(2,128)S(1)} %get-tuple-element.52), channel_id=1, replica_groups=mesh['tile_0'=4,'tile_1'=16,'tile_2'=2,'layer_0'=2,'layer_1'=2] {'layer_..., dimensions={0} | all-to-all | bytes 65536 | tf_op jit(solution)/shard_map/all_to_all | solution.py:622
  47.0 20.6 %all_to_all.11.parts = f32[16,2,128]{2,1,0:T(2,128)S(1)} all-to-all(f32[16,2,128]{2,1,0:T(2,128)S(1)} %shard_map.55), channel_id=1, replica_groups=mesh['tile_0'=4,'tile_1'=16,'tile_2'=2,'layer_0'=2,'layer_1'=2] {'tile_1'}, dimensions={0} | all-to-all | bytes 32768 | tf_op jit(solution)/shard_map/all_to_all | solution.py:624
  67.6 2.0 %shard_map.56 = (f32[384,128]{1,0:T(8,128)}, f32[384,128]{1,0:T(8,128)}) custom-call(f32[16,2,128]{2,1,0:T(2,128)S(1)} %all_to_all.11.parts, f32[24,6144]{1,0:T(8,128)S(1)} %get-tuple-element.53.block), custom_call_target="tpu_custom_call" | custom-call | tf_op jit(solution)/shard_map/pallas_call | solution.py:51
  (1 shorter events, 0.0 us)
Async XLA Ops:
  1.7 5.5 %collective-permute-start = (f32[13,8,128]{2,1,0:T(8,128)S(1)}, f32[13,8,128]{2,1,0:T(8,128)S(1)}, u32[]{:S(2)}, u32[]{:S(2)}) collective-permute-start(f32[13,8,128]{2,1,0:T(8,128)S(1)} %get-tuple-element.29), channel_id=1, source_target_pairs={{0,4},{4,0},{8,12},{12,8},{16,20},{20,16},{24,28},{28,24},{32,36},... | collective-permute-start | bytes 159752 | tf_op jit(solution)/shard_map/ppermute | solution.py:595
  5.7 1.5 %collective-permute-start.1 = (f32[13,8,128]{2,1,0:T(8,128)S(1)}, f32[13,8,128]{2,1,0:T(8,128)S(1)}, u32[]{:S(2)}, u32[]{:S(2)}) collective-permute-start(f32[13,8,128]{2,1,0:T(8,128)S(1)} %get-tuple-element.30), channel_id=1, source_target_pairs={{4,8},{8,4},{12,16},{16,12},{20,24},{24,20},{28,32},{32,28},{36,40... | collective-permute-start | bytes 159752 | tf_op jit(solution)/shard_map/ppermute | solution.py:594
  7.4 11.2 %collective-permute-start.3 = (f32[70,8,128]{2,1,0:T(8,128)S(1)}, f32[70,8,128]{2,1,0:T(8,128)S(1)}, u32[]{:S(2)}, u32[]{:S(2)}) collective-permute-start(f32[70,8,128]{2,1,0:T(8,128)S(1)} %get-tuple-element.44), channel_id=1, source_target_pairs={{0,1},{1,0},{2,3},{3,2},{4,5},{5,4},{6,7},{7,6},{8,9},{9,8},{10,11... | collective-permute-start | bytes 860168 | tf_op jit(solution)/shard_map/ppermute | solution.py:603
  16.7 9.5 %collective-permute-start.2 = (f32[70,8,128]{2,1,0:T(8,128)S(1)}, f32[70,8,128]{2,1,0:T(8,128)S(1)}, u32[]{:S(2)}, u32[]{:S(2)}) collective-permute-start(f32[70,8,128]{2,1,0:T(8,128)S(1)} %get-tuple-element.40), channel_id=1, source_target_pairs={{1,2},{2,1},{5,6},{6,5},{9,10},{10,9},{13,14},{14,13},{17,18},{18,... | collective-permute-start | bytes 860168 | tf_op jit(solution)/shard_map/ppermute | solution.py:602
